TPU v7x, 32 devices: a whole 2x2x4 slice. The times are simulated.
32 devices in a mesh: px: 8 (over z, y), py: 4 (over x, core).
Axes of the slice: x: 2, y: 2, z: 4, core: 2. Of those that a mesh axis runs over, the one named last changes fastest.
Arguments:
- spectrum: float32 [2, 1536, 24576], P(None, 'px', 'py'), may hold values from -6 to 6
- concentration: float32 [3072, 24576], P('px', 'py'), may hold values from -6 to 6
- factor_y: float32 [1536, 128], P('py'), may hold values from -0.15625 to 0.15625
- factor_x: float32 [3072, 256], P('px'), may hold values from -0.109375 to 0.109375
Outputs:
- y_compressed: float32 [16, 3072, 128], P('py', 'px')
- core_tensor: float32 [16, 256, 128], P('py', 'px')
All inputs are finite; a program needn't handle non-finite values.
Results may differ from a plain program's by a relative error of at most 0.000076.
Values sent between devices are 32-bit elements; how exact they have to be, the bound alone decides.
No kernel may reach another device: no remote copies, remote signals or barrier semaphores. Data moves between devices by JAX's collectives and lax.ppermute only.
A program may use at most 128 MiB of HBM per device.

v0:
```python
import functools
import math

import jax
import jax.numpy as jnp
from jax import lax
from jax.experimental import pallas as pl
from jax.experimental.pallas import tpu as pltpu
from jax.sharding import PartitionSpec as P


HIGHEST = lax.Precision.HIGHEST
LANES = 128


def exchange(value, axis, size, offset):
    return lax.ppermute(value, axis, [(a, a ^ offset) for a in range(size)])


def far_first(peers):
    half = peers // 2
    return list(range(half, peers)) + list(range(1, half))


def split_sets(sets):
    cut = max(1, sets // 2)
    out_groups = [g for g in (list(range(cut)), list(range(cut, sets))) if g]
    back_groups = [list(range(cut))] + [[j] for j in range(cut, sets)]
    return out_groups, back_groups


def synth_table(grid, modes, first_x, block_width):
    wave = lax.broadcasted_iota(jnp.int32, (modes, block_width), 0)
    column = first_x + lax.broadcasted_iota(jnp.int32, (modes, block_width), 1)
    phase = wave * column % grid
    angle = phase.astype(jnp.float32) * (2.0 * math.pi / grid)
    weight = jnp.where(wave == 0, 1.0, 2.0) / math.sqrt(modes)
    return jnp.concatenate([weight * jnp.cos(angle), -weight * jnp.sin(angle)], axis=0)


def general_body(px, spectrum, concentration, factor_y, factor_x):
    x_local, line_total = concentration.shape
    y_local = factor_y.shape[0]
    grid, modes = x_local * px, spectrum.shape[1] * px
    pencil = lax.all_to_all(spectrum, "px", split_axis=2, concat_axis=1, tiled=True)
    lines = pencil.shape[2]
    stacked = pencil.reshape(2 * modes, lines)

    def fill(block, velocity):
        rows = lax.dot_general(
            synth_table(grid, modes, block * x_local, x_local),
            stacked,
            (((0,), (0,)), ((), ())),
            precision=HIGHEST,
            preferred_element_type=jnp.float32,
        )
        return lax.dynamic_update_slice_in_dim(velocity, rows, block * x_local, 0)

    velocity = lax.fori_loop(0, px, fill, jnp.zeros((grid, lines), jnp.float32))
    returned = lax.all_to_all(velocity, "px", split_axis=0, concat_axis=1, tiled=True)
    flux = (returned * concentration).reshape(x_local, y_local, line_total // y_local)
    y_compressed = lax.psum_scatter(
        jnp.einsum("xyz,yr->zxr", flux, factor_y, precision=HIGHEST),
        "py",
        scatter_dimension=0,
        tiled=True,
    )
    terms = jnp.einsum("xs,zxr->zsr", factor_x, y_compressed, precision=HIGHEST)
    return y_compressed, lax.psum_scatter(terms, "px", scatter_dimension=1, tiled=True)


def pack_kernel(planes, groups, blocks_ref, in_ref, *refs):
    outs, turned = refs[:-1], refs[-1]
    turned[...] = in_ref[...].T
    count = turned.shape[0] // planes
    sets = sum(len(g) for g in groups)
    for out, group in zip(outs, groups):
        row = 0
        for j in group:
            for zb in range(planes // sets):
                part = turned[pl.ds(zb * sets + j, count, stride=planes), :]
                if len(out.shape) == 3:
                    out[0, row : row + count, :] = part
                else:
                    out[row : row + count, :] = part
                row += count


def pack_peer(value, block, width, planes, groups):
    rows = value.shape[0]
    sets = sum(len(g) for g in groups)
    shapes = [(width // sets * len(g), rows) for g in groups]
    return pl.pallas_call(
        functools.partial(pack_kernel, planes, groups),
        out_shape=[jax.ShapeDtypeStruct(s, value.dtype) for s in shapes],
        grid_spec=pltpu.PrefetchScalarGridSpec(
            num_scalar_prefetch=1,
            grid=(rows // LANES,),
            in_specs=[pl.BlockSpec((LANES, width), lambda i, b: (i, b[0]))],
            out_specs=[pl.BlockSpec((s[0], LANES), lambda i, b: (0, i)) for s in shapes],
            scratch_shapes=[pltpu.VMEM((width, LANES), value.dtype)],
        ),
        cost_estimate=pl.CostEstimate(flops=0, bytes_accessed=8 * rows * width, transcendentals=0),
        name="pack_peer",
    )(block, value)


def pack_all(value, blocks, width, planes, groups):
    rows, peers = value.shape[0], blocks.shape[0]
    sets = sum(len(g) for g in groups)
    shapes = [(peers, width // sets * len(g), rows) for g in groups]
    return pl.pallas_call(
        functools.partial(pack_kernel, planes, groups),
        out_shape=[jax.ShapeDtypeStruct(s, value.dtype) for s in shapes],
        grid_spec=pltpu.PrefetchScalarGridSpec(
            num_scalar_prefetch=1,
            grid=(peers, rows // LANES),
            in_specs=[pl.BlockSpec((LANES, width), lambda s, i, b: (i, b[s]))],
            out_specs=[pl.BlockSpec((1, s[1], LANES), lambda s, i, b: (s, 0, i)) for s in shapes],
            scratch_shapes=[pltpu.VMEM((width, LANES), value.dtype)],
        ),
        cost_estimate=pl.CostEstimate(
            flops=0, bytes_accessed=8 * rows * width * peers, transcendentals=0
        ),
        name="pack_all",
    )(blocks, value)


def table_kernel(cos_far, sin_far, cos_near, sin_near, out):
    k_local, tiles = cos_far.shape[1], cos_far.shape[2]

    @pl.loop(0, k_local // 8)
    def _(step):
        row = pl.multiple_of(step * 8, 8)
        far_c, far_s = cos_far[0, pl.ds(row, 8), :], sin_far[0, pl.ds(row, 8), :]
        near_c, near_s = cos_near[0, pl.ds(row, 8), :], sin_near[0, pl.ds(row, 8), :]
        for u in range(tiles):
            c, s = far_c[:, u : u + 1], far_s[:, u : u + 1]
            lanes = slice(u * LANES, (u + 1) * LANES)
            out[pl.ds(row, 8), lanes] = c * near_c - s * near_s
            out[pl.ds(pl.multiple_of(k_local + row, 8), 8), lanes] = -(s * near_c + c * near_s)


def build_table(blocks, k_local, x_local):
    peers = blocks.shape[0]
    grid, modes = x_local * peers, k_local * peers
    wave = blocks[:, None] * k_local + jnp.arange(k_local, dtype=jnp.int32)[None, :]
    starts = jnp.arange(x_local // LANES, dtype=jnp.int32) * LANES
    far = (blocks[:, None] * x_local + starts[None, :]).reshape(-1)
    near = jnp.arange(LANES, dtype=jnp.int32)

    def angle(column):
        phase = wave[:, :, None] * column[None, None, :] % grid
        return phase.astype(jnp.float32) * (2.0 * math.pi / grid)

    weight = (jnp.where(wave == 0, 1.0, 2.0) / math.sqrt(modes)).astype(jnp.float32)[:, :, None]
    tables = (
        jnp.cos(angle(far)),
        jnp.sin(angle(far)),
        weight * jnp.cos(angle(near)),
        weight * jnp.sin(angle(near)),
    )
    size = 2 * k_local * peers * grid
    return pl.pallas_call(
        table_kernel,
        out_shape=jax.ShapeDtypeStruct((2 * modes, grid), jnp.float32),
        grid=(peers,),
        in_specs=[pl.BlockSpec((1,) + t.shape[1:], lambda s: (s, 0, 0)) for t in tables],
        out_specs=pl.BlockSpec((2 * k_local, grid), lambda s: (s, 0)),
        cost_estimate=pl.CostEstimate(flops=3 * size, bytes_accessed=4 * size, transcendentals=0),
        name="build_table",
    )(*tables)


def flux_kernel(peers, index_ref, *refs):
    v_refs, (c_ref, fy_ref, out, flux) = refs[:peers], refs[peers:]
    count = c_ref.shape[1]
    for s in range(peers):
        flux[s * count : (s + 1) * count, :] = v_refs[s][...] * c_ref[s]
    out[0] = jnp.dot(
        fy_ref[...], flux[...], precision=HIGHEST, preferred_element_type=jnp.float32
    )


def contract_flux(parts, place, conc, factor, me_y, owners):
    peers, rows, x_local = conc.shape
    count = rows // owners
    rank, y_local = factor.shape
    return pl.pallas_call(
        functools.partial(flux_kernel, peers),
        out_shape=jax.ShapeDtypeStruct((owners, rank, x_local), jnp.float32),
        grid_spec=pltpu.PrefetchScalarGridSpec(
            num_scalar_prefetch=1,
            grid=(owners,),
            in_specs=[
                pl.BlockSpec((count, x_local), lambda t, m: (place * owners + (m[0] ^ t), 0))
                for _ in parts
            ]
            + [
                pl.BlockSpec((peers, count, x_local), lambda t, m: (0, m[0] ^ t, 0)),
                pl.BlockSpec((rank, y_local), lambda t, m: (0, 0)),
            ],
            out_specs=pl.BlockSpec((1, rank, x_local), lambda t, m: (t, 0, 0)),
            scratch_shapes=[pltpu.VMEM((y_local, x_local), jnp.float32)],
        ),
        cost_estimate=pl.CostEstimate(
            flops=2 * owners * rank * y_local * x_local,
            bytes_accessed=8 * peers * rows * x_local,
            transcendentals=0,
        ),
        name="contract_flux",
    )(me_y, *parts, conc, factor)


def aligned_body(px, py, spectrum, concentration, factor_y, factor_x):
    k_local = spectrum.shape[1]
    x_local, line_total = concentration.shape
    y_local, rank = factor_y.shape
    planes = line_total // y_local
    sets = planes // py
    width = line_total // px
    y_peer = y_local // px
    me_x = lax.axis_index("px").astype(jnp.int32)
    me_y = lax.axis_index("py").astype(jnp.int32).reshape(1)
    blocks = me_x ^ jnp.arange(px, dtype=jnp.int32)
    order = far_first(px)
    stacked = spectrum.reshape(2 * k_local, line_total)
    out_groups, back_groups = split_sets(sets)

    packed = {s: pack_peer(stacked, blocks[s : s + 1], width, planes, out_groups) for s in order + [0]}
    arrived = []
    for g in range(len(out_groups)):
        got = {s: exchange(packed[s][g], "px", px, s) for s in order}
        got[0] = packed[0][g]
        arrived.append(got)

    table = build_table(blocks, k_local, x_local)
    conc = pack_all(concentration, blocks, width, planes, [[j] for j in range(sets)])
    factor = jnp.concatenate(
        [lax.dynamic_slice_in_dim(factor_y, blocks[s] * y_peer, y_peer, 0) for s in range(px)], axis=0
    ).T

    rows_set = y_peer * py
    velocity = {}
    for group, got in zip(out_groups, arrived):
        lines = jnp.concatenate([got[s] for s in range(px)], axis=1)
        whole = lax.dot_general(
            lines,
            table,
            (((1,), (0,)), ((), ())),
            precision=lax.Precision.HIGH,
            preferred_element_type=jnp.float32,
        )
        for at, j in enumerate(group):
            velocity[j] = (whole, at)

    y_parts, core_parts = [], []
    for group in back_groups:
        whole, first = velocity[group[0]]
        rows = slice(first * rows_set, (first + len(group)) * rows_set)
        own = whole[rows]
        parts = [None] * px
        parts[0] = own[:, :x_local]
        for s in order:
            parts[s] = exchange(own[:, s * x_local : (s + 1) * x_local], "px", px, s)
        cores = []
        for place, j in enumerate(group):
            sums = contract_flux(parts, place, conc[j], factor, me_y, py)
            total = sums[0]
            for t in range(1, py):
                total = total + exchange(sums[t], "py", py, t)
            y_parts.append(total.T)
            cores.append(
                lax.dot_general(
                    factor_x,
                    total,
                    (((0,), (1,)), ((), ())),
                    precision=HIGHEST,
                    preferred_element_type=jnp.float32,
                )
            )
        s_local = factor_x.shape[1] // px
        terms = jnp.stack(cores).reshape(len(group), px, s_local, rank).transpose(1, 0, 2, 3)
        terms = lax.all_to_all(terms, "px", split_axis=0, concat_axis=0, tiled=True)
        core_parts.append(jnp.sum(terms, axis=0))
    return jnp.stack(y_parts), jnp.concatenate(core_parts, axis=0)


def is_aligned(px, py, spectrum, concentration, factor_y):
    x_local, line_total = concentration.shape[0] // px, concentration.shape[1] // py
    y_local, k_local = factor_y.shape[0] // py, spectrum.shape[1] // px
    planes = line_total // y_local
    return (
        px > 1
        and px & (px - 1) == 0
        and py & (py - 1) == 0
        and planes % py == 0
        and planes % 8 == 0
        and planes // py > 1
        and (line_total // px) % LANES == 0
        and x_local % LANES == 0
        and y_local % (8 * px) == 0
        and k_local * 2 == x_local
        and k_local % 8 == 0
    )


def solution(mesh):
    px, py = mesh.shape["px"], mesh.shape["py"]
    placed = (P(None, "px", "py"), P("px", "py"), P("py", None), P("px", None))
    shard = functools.partial(
        jax.shard_map,
        mesh=mesh,
        in_specs=placed,
        out_specs=(P("py", "px", None), P("py", "px", None)),
        check_vma=False,
    )

    def step(spectrum, concentration, factor_y, factor_x):
        args = (spectrum, concentration, factor_y, factor_x)
        if not is_aligned(px, py, spectrum, concentration, factor_y):
            return shard(functools.partial(general_body, px))(*args)

        def body(*blocks):
            return aligned_body(px, py, *blocks)

        return shard(body)(*args)

    return step
```

profile of v0, /device:TPU:0, one launch (start us, length us, event | category | flops | bytes accessed | tf_op | source)
XLA Modules:
  0.0 547.3 jit_solution(5510376146025050613)
XLA Ops:
  34.8 5.1 sine_multiply_fusion
  57.8 18.8 %pack_all.1 = (f32[8,192,384]{2,1,0:T(8,128)}, f32[8,192,384]{2,1,0:T(8,128)}, f32[8,192,384]{2,1,0:T(8,128)}, f32[8,192,384]{2,1,0:T(8,128)}) custom-call(s32[8]{0:T(128)} %copy-done.26, f32[384,6144]{1,0:T(8,128)} %in_ref.1), custom_call_target="tpu_custom_call" | custom-call | bytes 18874368 | tf_op jit(solution)/shard_map/pack_all/pallas_call | solution.py:112
  77.5 31.8 %build_table.1 = f32[3072,3072]{1,0:T(8,128)} custom-call(f32[8,192,24]{2,1,0:T(8,128)} %get-tuple-element.87.cos_far, f32[8,192,24]{2,1,0:T(8,128)} %get-tuple-element.86.sin_far, f32[8,192,128]{2,1,0:T(8,128)} %get-tuple-element.97.cos_near, f32[8,192,128]{2,1,0:T(8,128)} %get-tuple-element.96.sin_near), custom_call_target="tpu_custom_call" | custom-call | flops 28311552 | bytes 37748736 | tf_op jit(solution)/shard_map/build_table/pallas_call | solution.py:164
  130.7 25.4 %collective-permute-start.3 = (f32[384,384]{1,0:T(8,128)S(1)}, f32[384,384]{1,0:T(8,128)S(1)}, u32[]{:S(2)}, u32[]{:S(2)}) collective-permute-start(f32[384,384]{1,0:T(8,128)S(1)} %copy-done.28), channel_id=1, source_target_pairs={{0,16},{4,20},{8,24},{12,28},{16,0},{20,4},{24,8},{28,12},{1,17},{... | collective-permute-start | bytes 1769480 | tf_op jit(solution)/shard_map/ppermute | solution.py:17
  156.9 35.5 %collective-permute-start.4 = (f32[384,384]{1,0:T(8,128)S(1)}, f32[384,384]{1,0:T(8,128)S(1)}, u32[]{:S(2)}, u32[]{:S(2)}) collective-permute-start(f32[384,384]{1,0:T(8,128)S(1)} %copy-done.27), channel_id=1, source_target_pairs={{0,20},{4,16},{8,28},{12,24},{16,4},{20,0},{24,12},{28,8},{1,21},{... | collective-permute-start | bytes 1769480 | tf_op jit(solution)/shard_map/ppermute | solution.py:17
  193.4 30.1 %fusion.25 = f32[384,3072]{1,0:T(8,128)S(1)} fusion(f32[384,3072]{1,0:T(8,128)} %constant_dynamic-update-slice_fusion.8, f32[3072,3072]{1,0:T(8,128)} %build_table.1), kind=kOutput, calls=%fused_computation.87 | convolution fusion | flops 21743271936 | bytes 47185920 | tf_op jit(solution)/shard_map/dot_general | solution.py:247
  232.3 17.6 %collective-permute-done.4 = f32[384,384]{1,0:T(8,128)S(1)} collective-permute-done((f32[384,384]{1,0:T(8,128)S(1)}, f32[384,384]{1,0:T(8,128)S(1)}, u32[]{:S(2)}, u32[]{:S(2)}) %collective-permute-start.4) | collective-permute-done | bytes 589856 | tf_op jit(solution)/shard_map/ppermute | solution.py:17
  250.1 17.7 %collective-permute-start.30 = (f32[192,384]{1,0:T(8,128)S(1)}, f32[192,384]{1,0:T(8,128)S(1)}, u32[]{:S(2)}, u32[]{:S(2)}) collective-permute-start(f32[192,384]{1,0:T(8,128)S(1)} %get-tuple-element.69), channel_id=1, source_target_pairs={{0,16},{4,20},{8,24},{12,28},{16,0},{20,4},{24,8},{28,12},{1,17},{... | collective-permute-start | bytes 884744 | tf_op jit(solution)/shard_map/ppermute | solution.py:17
  268.0 16.5 %collective-permute-start.31 = (f32[192,384]{1,0:T(8,128)S(1)}, f32[192,384]{1,0:T(8,128)S(1)}, u32[]{:S(2)}, u32[]{:S(2)}) collective-permute-start(f32[192,384]{1,0:T(8,128)S(1)} %get-tuple-element.68), channel_id=1, source_target_pairs={{0,20},{4,16},{8,28},{12,24},{16,4},{20,0},{24,12},{28,8},{1,21},{... | collective-permute-start | bytes 884744 | tf_op jit(solution)/shard_map/ppermute | solution.py:17
  290.0 16.6 %collective-permute-done.30.refs_4_ = f32[192,384]{1,0:T(8,128)S(1)} collective-permute-done((f32[192,384]{1,0:T(8,128)S(1)}, f32[192,384]{1,0:T(8,128)S(1)}, u32[]{:S(2)}, u32[]{:S(2)}) %collective-permute-start.30) | collective-permute-done | bytes 294944 | tf_op jit(solution)/shard_map/ppermute | solution.py:17
  307.0 29.8 %fusion.24 = f32[384,3072]{1,0:T(8,128)S(1)} fusion(f32[384,3072]{1,0:T(8,128)} %copy-done.25, f32[3072,3072]{1,0:T(8,128)} %build_table.1), kind=kOutput, calls=%fused_computation.86 | convolution fusion | flops 21743271936 | bytes 47185920 | tf_op jit(solution)/shard_map/dot_general | solution.py:247
  348.8 5.5 %contract_flux.6 = f32[4,128,384]{2,1,0:T(8,128)} custom-call(s32[1]{0:T(128)} %bitcast.index_ref, f32[192,384]{1,0:T(8,128)} %get-tuple-element.73.refs_0_, f32[192,384]{1,0:T(8,128)} %copy-done.9, f32[192,384]{1,0:T(8,128)} %copy-done.10, f32[192,384]{1,0:T(8,128)} %copy-done.12, f32[192,384]{1,0:T(8,128)} %copy-done.14, f32[192,384]{1,0:T(8,128)} %copy-done.17, ...), custom_call_target="tpu_custom_call" | custom-call | flops 150994944 | bytes 4718592 | tf_op jit(solution)/shard_map/contract_flux/pallas_call | solution.py:189
  354.4 44.0 %collective-permute-done.40.refs_4_ = f32[192,384]{1,0:T(8,128)S(1)} collective-permute-done((f32[192,384]{1,0:T(8,128)S(1)}, f32[192,384]{1,0:T(8,128)S(1)}, u32[]{:S(2)}, u32[]{:S(2)}) %collective-permute-start.40) | collective-permute-done | bytes 294944 | tf_op jit(solution)/shard_map/ppermute | solution.py:17
  400.5 5.2 collective-permute-done.41.refs_5_
  407.6 5.5 %contract_flux.7 = f32[4,128,384]{2,1,0:T(8,128)} custom-call(s32[1]{0:T(128)} %bitcast.index_ref, f32[192,384]{1,0:T(8,128)} %get-tuple-element.66.refs_0_, f32[192,384]{1,0:T(8,128)} %copy-done.11, f32[192,384]{1,0:T(8,128)} %copy-done.13, f32[192,384]{1,0:T(8,128)} %copy-done.15, f32[192,384]{1,0:T(8,128)} %copy-done.16, ...), custom_call_target="tpu_custom_call" | custom-call | flops 150994944 | bytes 4718592 | tf_op jit(solution)/shard_map/contract_flux/pallas_call | solution.py:189
  429.2 26.1 %collective-permute-done.10.refs_4_ = f32[384,384]{1,0:T(8,128)S(1)} collective-permute-done((f32[384,384]{1,0:T(8,128)}, f32[384,384]{1,0:T(8,128)S(1)}, u32[]{:S(2)}, u32[]{:S(2)}) %collective-permute-start.10) | collective-permute-done | bytes 589856 | tf_op jit(solution)/shard_map/ppermute | solution.py:17
  456.6 12.2 %collective-permute-done.11.refs_5_ = f32[384,384]{1,0:T(8,128)S(1)} collective-permute-done((f32[384,384]{1,0:T(8,128)}, f32[384,384]{1,0:T(8,128)S(1)}, u32[]{:S(2)}, u32[]{:S(2)}) %collective-permute-start.11) | collective-permute-done | bytes 589856 | tf_op jit(solution)/shard_map/ppermute | solution.py:17
  472.7 5.4 all-to-all-start.1
  482.8 10.6 %collective-permute-done.9.refs_3_ = f32[384,384]{1,0:T(8,128)} collective-permute-done((f32[384,384]{1,0:T(8,128)}, f32[384,384]{1,0:T(8,128)}, u32[]{:S(2)}, u32[]{:S(2)}) %collective-permute-start.9) | collective-permute-done | bytes 589856 | tf_op jit(solution)/shard_map/ppermute | solution.py:17
  493.4 5.5 %contract_flux.4 = f32[4,128,384]{2,1,0:T(8,128)} custom-call(s32[1]{0:T(128)} %bitcast.index_ref, f32[384,384]{1,0:T(8,128)} %get-tuple-element.57.refs_0_, f32[384,384]{1,0:T(8,128)} %copy-done.5, f32[384,384]{1,0:T(8,128)} %collective-permute-done.8.refs_2_, f32[384,384]{1,0:T(8,128)} %collective-permute-done.9.refs_3_, f32[384,384]{1,0:T(8,128)} %copy-done.1, ...), custom_call_target="tpu_custom_call" | custom-call | flops 150994944 | bytes 4718592 | tf_op jit(solution)/shard_map/contract_flux/pallas_call | solution.py:189
  502.0 5.4 contract_flux.5
  520.8 6.2 %all-to-all-start.2 = ((f32[8,1,32,128]{3,2,1,0:T(8,128)}), f32[8,1,32,128]{3,2,1,0:T(8,128)S(1)}, u32[]{:S(2)}, u32[]{:S(2)}) async-start(f32[8,1,32,128]{3,2,1,0:T(8,128)} %bitcast.46), calls=%async_computation.2 | async-start | bytes 262144 | tf_op jit(solution)/shard_map/all_to_all | solution.py:284
  528.3 6.5 %all-to-all-done.2 = f32[8,1,32,128]{3,2,1,0:T(8,128)S(1)} async-done(((f32[8,1,32,128]{3,2,1,0:T(8,128)}), f32[8,1,32,128]{3,2,1,0:T(8,128)S(1)}, u32[]{:S(2)}, u32[]{:S(2)}) %all-to-all-start.2) | async-done | bytes 131104 | tf_op jit(solution)/shard_map/all_to_all | solution.py:284
  540.4 6.3 %all-to-all-done = f32[8,2,32,128]{3,2,1,0:T(8,128)S(1)} async-done(((f32[8,2,32,128]{3,2,1,0:T(8,128)}), f32[8,2,32,128]{3,2,1,0:T(8,128)S(1)}, u32[]{:S(2)}, u32[]{:S(2)}) %all-to-all-start) | async-done | bytes 262176 | tf_op jit(solution)/shard_map/all_to_all | solution.py:284
  (227 shorter events, 151.6 us)
Async XLA Ops:
  5.3 107.0 %collective-permute-start.20 = (f32[384,384]{1,0:T(8,128)}, f32[384,384]{1,0:T(8,128)}, u32[]{:S(2)}, u32[]{:S(2)}) collective-permute-start(f32[384,384]{1,0:T(8,128)} %get-tuple-element.33), channel_id=1, source_target_pairs={{0,4},{4,0},{8,12},{12,8},{16,20},{20,16},{24,28},{28,24},{1,5},{5... | collective-permute-start | bytes 1769480 | tf_op jit(solution)/shard_map/ppermute | solution.py:17
  12.3 105.5 %collective-permute-start.21 = (f32[384,384]{1,0:T(8,128)}, f32[384,384]{1,0:T(8,128)}, u32[]{:S(2)}, u32[]{:S(2)}) collective-permute-start(f32[384,384]{1,0:T(8,128)} %get-tuple-element.34), channel_id=1, source_target_pairs={{0,8},{4,12},{8,0},{12,4},{16,24},{20,28},{24,16},{28,20},{1,9},{5... | collective-permute-start | bytes 1769480 | tf_op jit(solution)/shard_map/ppermute | solution.py:17
  17.9 101.9 %collective-permute-start.22 = (f32[384,384]{1,0:T(8,128)}, f32[384,384]{1,0:T(8,128)S(1)}, u32[]{:S(2)}, u32[]{:S(2)}) collective-permute-start(f32[384,384]{1,0:T(8,128)} %get-tuple-element.35), channel_id=1, source_target_pairs={{0,12},{4,8},{8,4},{12,0},{16,28},{20,24},{24,20},{28,16},{1,13},{... | collective-permute-start | bytes 1769480 | tf_op jit(solution)/shard_map/ppermute | solution.py:17
  22.0 100.4 %collective-permute-start.23 = (f32[384,384]{1,0:T(8,128)}, f32[384,384]{1,0:T(8,128)S(1)}, u32[]{:S(2)}, u32[]{:S(2)}) collective-permute-start(f32[384,384]{1,0:T(8,128)} %get-tuple-element.36), channel_id=1, source_target_pairs={{0,16},{4,20},{8,24},{12,28},{16,0},{20,4},{24,8},{28,12},{1,17},{... | collective-permute-start | bytes 1769480 | tf_op jit(solution)/shard_map/ppermute | solution.py:17
  29.1 94.2 %collective-permute-start.24 = (f32[384,384]{1,0:T(8,128)}, f32[384,384]{1,0:T(8,128)S(1)}, u32[]{:S(2)}, u32[]{:S(2)}) collective-permute-start(f32[384,384]{1,0:T(8,128)} %get-tuple-element.37), channel_id=1, source_target_pairs={{0,20},{4,16},{8,28},{12,24},{16,4},{20,0},{24,12},{28,8},{1,21},{... | collective-permute-start | bytes 1769480 | tf_op jit(solution)/shard_map/ppermute | solution.py:17
  119.8 103.7 %collective-permute-start = (f32[384,384]{1,0:T(8,128)S(1)}, f32[384,384]{1,0:T(8,128)S(1)}, u32[]{:S(2)}, u32[]{:S(2)}) collective-permute-start(f32[384,384]{1,0:T(8,128)S(1)} %copy-done.31), channel_id=1, source_target_pairs={{0,4},{4,0},{8,12},{12,8},{16,20},{20,16},{24,28},{28,24},{1,5},{5... | collective-permute-start | bytes 1769480 | tf_op jit(solution)/shard_map/ppermute | solution.py:17
  122.4 106.6 %collective-permute-start.1 = (f32[384,384]{1,0:T(8,128)S(1)}, f32[384,384]{1,0:T(8,128)S(1)}, u32[]{:S(2)}, u32[]{:S(2)}) collective-permute-start(f32[384,384]{1,0:T(8,128)S(1)} %copy-done.30), channel_id=1, source_target_pairs={{0,8},{4,12},{8,0},{12,4},{16,24},{20,28},{24,16},{28,20},{1,9},{5... | collective-permute-start | bytes 1769480 | tf_op jit(solution)/shard_map/ppermute | solution.py:17
  123.3 107.5 %collective-permute-start.2 = (f32[384,384]{1,0:T(8,128)S(1)}, f32[384,384]{1,0:T(8,128)S(1)}, u32[]{:S(2)}, u32[]{:S(2)}) collective-permute-start(f32[384,384]{1,0:T(8,128)S(1)} %copy-done.29), channel_id=1, source_target_pairs={{0,12},{4,8},{8,4},{12,0},{16,28},{20,24},{24,20},{28,16},{1,13},{... | collective-permute-start | bytes 1769480 | tf_op jit(solution)/shard_map/ppermute | solution.py:17
  130.7 101.5 %collective-permute-start.3 = (f32[384,384]{1,0:T(8,128)S(1)}, f32[384,384]{1,0:T(8,128)S(1)}, u32[]{:S(2)}, u32[]{:S(2)}) collective-permute-start(f32[384,384]{1,0:T(8,128)S(1)} %copy-done.28), channel_id=1, source_target_pairs={{0,16},{4,20},{8,24},{12,28},{16,0},{20,4},{24,8},{28,12},{1,17},{... | collective-permute-start | bytes 1769480 | tf_op jit(solution)/shard_map/ppermute | solution.py:17
  156.9 93.0 %collective-permute-start.4 = (f32[384,384]{1,0:T(8,128)S(1)}, f32[384,384]{1,0:T(8,128)S(1)}, u32[]{:S(2)}, u32[]{:S(2)}) collective-permute-start(f32[384,384]{1,0:T(8,128)S(1)} %copy-done.27), channel_id=1, source_target_pairs={{0,20},{4,16},{8,28},{12,24},{16,4},{20,0},{24,12},{28,8},{1,21},{... | collective-permute-start | bytes 1769480 | tf_op jit(solution)/shard_map/ppermute | solution.py:17
  250.1 56.5 %collective-permute-start.30 = (f32[192,384]{1,0:T(8,128)S(1)}, f32[192,384]{1,0:T(8,128)S(1)}, u32[]{:S(2)}, u32[]{:S(2)}) collective-permute-start(f32[192,384]{1,0:T(8,128)S(1)} %get-tuple-element.69), channel_id=1, source_target_pairs={{0,16},{4,20},{8,24},{12,28},{16,0},{20,4},{24,8},{28,12},{1,17},{... | collective-permute-start | bytes 884744 | tf_op jit(solution)/shard_map/ppermute | solution.py:17
  268.0 68.9 %collective-permute-start.31 = (f32[192,384]{1,0:T(8,128)S(1)}, f32[192,384]{1,0:T(8,128)S(1)}, u32[]{:S(2)}, u32[]{:S(2)}) collective-permute-start(f32[192,384]{1,0:T(8,128)S(1)} %get-tuple-element.68), channel_id=1, source_target_pairs={{0,20},{4,16},{8,28},{12,24},{16,4},{20,0},{24,12},{28,8},{1,21},{... | collective-permute-start | bytes 884744 | tf_op jit(solution)/shard_map/ppermute | solution.py:17
  284.6 54.2 %collective-permute-start.32 = (f32[192,384]{1,0:T(8,128)S(1)}, f32[192,384]{1,0:T(8,128)S(1)}, u32[]{:S(2)}, u32[]{:S(2)}) collective-permute-start(f32[192,384]{1,0:T(8,128)S(1)} %get-tuple-element.67), channel_id=1, source_target_pairs={{0,24},{4,28},{8,16},{12,20},{16,8},{20,12},{24,0},{28,4},{1,25},{... | collective-permute-start | bytes 884744 | tf_op jit(solution)/shard_map/ppermute | solution.py:17
  285.3 55.2 %collective-permute-start.33 = (f32[192,384]{1,0:T(8,128)S(1)}, f32[192,384]{1,0:T(8,128)S(1)}, u32[]{:S(2)}, u32[]{:S(2)}) collective-permute-start(f32[192,384]{1,0:T(8,128)S(1)} %get-tuple-element.58), channel_id=1, source_target_pairs={{0,28},{4,24},{8,20},{12,16},{16,12},{20,8},{24,4},{28,0},{1,29},{... | collective-permute-start | bytes 884744 | tf_op jit(solution)/shard_map/ppermute | solution.py:17
  288.5 53.9 %collective-permute-start.37 = (f32[192,384]{1,0:T(8,128)S(1)}, f32[192,384]{1,0:T(8,128)S(1)}, u32[]{:S(2)}, u32[]{:S(2)}) collective-permute-start(f32[192,384]{1,0:T(8,128)S(1)} %get-tuple-element.65), channel_id=1, source_target_pairs={{0,4},{4,0},{8,12},{12,8},{16,20},{20,16},{24,28},{28,24},{1,5},{5... | collective-permute-start | bytes 884744 | tf_op jit(solution)/shard_map/ppermute | solution.py:17
  338.9 59.5 %collective-permute-start.40 = (f32[192,384]{1,0:T(8,128)S(1)}, f32[192,384]{1,0:T(8,128)S(1)}, u32[]{:S(2)}, u32[]{:S(2)}) collective-permute-start(f32[192,384]{1,0:T(8,128)S(1)} %get-tuple-element.62), channel_id=1, source_target_pairs={{0,16},{4,20},{8,24},{12,28},{16,0},{20,4},{24,8},{28,12},{1,17},{... | collective-permute-start | bytes 884744 | tf_op jit(solution)/shard_map/ppermute | solution.py:17
  340.6 65.1 %collective-permute-start.41 = (f32[192,384]{1,0:T(8,128)S(1)}, f32[192,384]{1,0:T(8,128)}, u32[]{:S(2)}, u32[]{:S(2)}) collective-permute-start(f32[192,384]{1,0:T(8,128)S(1)} %get-tuple-element.61), channel_id=1, source_target_pairs={{0,20},{4,16},{8,28},{12,24},{16,4},{20,0},{24,12},{28,8},{1,21},{... | collective-permute-start | bytes 884744 | tf_op jit(solution)/shard_map/ppermute | solution.py:17
  342.5 63.2 %collective-permute-start.42 = (f32[192,384]{1,0:T(8,128)S(1)}, f32[192,384]{1,0:T(8,128)}, u32[]{:S(2)}, u32[]{:S(2)}) collective-permute-start(f32[192,384]{1,0:T(8,128)S(1)} %get-tuple-element.60), channel_id=1, source_target_pairs={{0,24},{4,28},{8,16},{12,20},{16,8},{20,12},{24,0},{28,4},{1,25},{... | collective-permute-start | bytes 884744 | tf_op jit(solution)/shard_map/ppermute | solution.py:17
  345.8 61.4 %collective-permute-start.43 = (f32[192,384]{1,0:T(8,128)S(1)}, f32[192,384]{1,0:T(8,128)}, u32[]{:S(2)}, u32[]{:S(2)}) collective-permute-start(f32[192,384]{1,0:T(8,128)S(1)} %get-tuple-element.59), channel_id=1, source_target_pairs={{0,28},{4,24},{8,20},{12,16},{16,12},{20,8},{24,4},{28,0},{1,29},{... | collective-permute-start | bytes 884744 | tf_op jit(solution)/shard_map/ppermute | solution.py:17
  354.3 101.0 %collective-permute-start.10 = (f32[384,384]{1,0:T(8,128)}, f32[384,384]{1,0:T(8,128)S(1)}, u32[]{:S(2)}, u32[]{:S(2)}) collective-permute-start(f32[384,384]{1,0:T(8,128)} %get-tuple-element.53), channel_id=1, source_target_pairs={{0,16},{4,20},{8,24},{12,28},{16,0},{20,4},{24,8},{28,12},{1,17},{... | collective-permute-start | bytes 1769480 | tf_op jit(solution)/shard_map/ppermute | solution.py:17
  398.4 70.5 %collective-permute-start.11 = (f32[384,384]{1,0:T(8,128)}, f32[384,384]{1,0:T(8,128)S(1)}, u32[]{:S(2)}, u32[]{:S(2)}) collective-permute-start(f32[384,384]{1,0:T(8,128)} %get-tuple-element.52), channel_id=1, source_target_pairs={{0,20},{4,16},{8,28},{12,24},{16,4},{20,0},{24,12},{28,8},{1,21},{... | collective-permute-start | bytes 1769480 | tf_op jit(solution)/shard_map/ppermute | solution.py:17
  420.1 62.7 %collective-permute-start.12 = (f32[384,384]{1,0:T(8,128)}, f32[384,384]{1,0:T(8,128)S(1)}, u32[]{:S(2)}, u32[]{:S(2)}) collective-permute-start(f32[384,384]{1,0:T(8,128)} %get-tuple-element.51), channel_id=1, source_target_pairs={{0,24},{4,28},{8,16},{12,20},{16,8},{20,12},{24,0},{28,4},{1,25},{... | collective-permute-start | bytes 1769480 | tf_op jit(solution)/shard_map/ppermute | solution.py:17
  424.6 58.2 %collective-permute-start.13 = (f32[384,384]{1,0:T(8,128)}, f32[384,384]{1,0:T(8,128)S(1)}, u32[]{:S(2)}, u32[]{:S(2)}) collective-permute-start(f32[384,384]{1,0:T(8,128)} %get-tuple-element.50), channel_id=1, source_target_pairs={{0,28},{4,24},{8,20},{12,16},{16,12},{20,8},{24,4},{28,0},{1,29},{... | collective-permute-start | bytes 1769480 | tf_op jit(solution)/shard_map/ppermute | solution.py:17
  427.7 55.1 %collective-permute-start.7 = (f32[384,384]{1,0:T(8,128)}, f32[384,384]{1,0:T(8,128)S(1)}, u32[]{:S(2)}, u32[]{:S(2)}) collective-permute-start(f32[384,384]{1,0:T(8,128)} %get-tuple-element.56), channel_id=1, source_target_pairs={{0,4},{4,0},{8,12},{12,8},{16,20},{20,16},{24,28},{28,24},{1,5},{5... | collective-permute-start | bytes 1769480 | tf_op jit(solution)/shard_map/ppermute | solution.py:17
  (61 other events, 1624.0 us)
where the time goes:
time: 549 us; the launch traced here: 547 us
  starting transfers between devices  168 us (31%)
  waiting for transfers between devices  158 us (29%)
  Pallas kernels  105 us (19%)
  matrix products  62.8 us (11%)
  local copies, waits for them, and re-layouts  31.8 us (6%)
  other arithmetic  15.2 us (3%)
  between operations  6.23 us (1%)
    ppermute x47, starting transfers between devices, exchange(): return lax.ppermute(value, axis, [(a, a ^ offset) for a in range(size)])  153 us
    ppermute x47, waiting for transfers between devices, exchange(): return lax.ppermute(value, axis, [(a, a ^ offset) for a in range(size)])  145 us
    dot_general x2, matrix products, aligned_body(): lax.dot_general(lines, table, (((1,), (0,)), ((), ())), precision=lax.Pre...  59.9 us
    pallas_call x8, Pallas kernels, pack_peer(): pl.pallas_call(functools.partial(pack_kernel, planes, groups), out_shape=...  32.4 us
    pallas_call x1, Pallas kernels, build_table(): pl.pallas_call(table_kernel, out_shape=jax.ShapeDtypeStruct((2 * modes, g...  31.8 us
    pallas_call x4, Pallas kernels, contract_flux(): pl.pallas_call(functools.partial(flux_kernel, peers), out_shape=jax.Shape...  21.9 us
    pallas_call x1, Pallas kernels, pack_all(): pl.pallas_call(functools.partial(pack_kernel, planes, groups), out_shape=...  18.8 us
    unnamed x93, local copies, waits for them, and re-layouts  15.9 us
  transfers between devices with their start and end apart: 50, of which 14 were waited for; matrix products, arithmetic and copies ran while one was open for 19% of the time, Pallas kernels for 18%

commit v1 on v0

--- a/solution.py
+++ b/solution.py
@@ -173,13 +173,16 @@
 
 
 def flux_kernel(peers, index_ref, *refs):
-    v_refs, (c_ref, fy_ref, out, flux) = refs[:peers], refs[peers:]
+    v_refs, (c_ref, fy_ref, *outs, flux) = refs[:peers], refs[peers:]
     count = c_ref.shape[1]
     for s in range(peers):
         flux[s * count : (s + 1) * count, :] = v_refs[s][...] * c_ref[s]
-    out[0] = jnp.dot(
-        fy_ref[...], flux[...], precision=HIGHEST, preferred_element_type=jnp.float32
-    )
+    sums = jnp.dot(fy_ref[...], flux[...], precision=HIGHEST, preferred_element_type=jnp.float32)
+    for t, out in enumerate(outs):
+
+        @pl.when(pl.program_id(0) == t)
+        def _(out=out):
+            out[...] = sums
 
 
 def contract_flux(parts, place, conc, factor, me_y, owners):
@@ -188,7 +191,7 @@
     rank, y_local = factor.shape
     return pl.pallas_call(
         functools.partial(flux_kernel, peers),
-        out_shape=jax.ShapeDtypeStruct((owners, rank, x_local), jnp.float32),
+        out_shape=[jax.ShapeDtypeStruct((rank, x_local), jnp.float32)] * owners,
         grid_spec=pltpu.PrefetchScalarGridSpec(
             num_scalar_prefetch=1,
             grid=(owners,),
@@ -200,7 +203,7 @@
                 pl.BlockSpec((peers, count, x_local), lambda t, m: (0, m[0] ^ t, 0)),
                 pl.BlockSpec((rank, y_local), lambda t, m: (0, 0)),
             ],
-            out_specs=pl.BlockSpec((1, rank, x_local), lambda t, m: (t, 0, 0)),
+            out_specs=[pl.BlockSpec((rank, x_local), lambda t, m: (0, 0))] * owners,
             scratch_shapes=[pltpu.VMEM((y_local, x_local), jnp.float32)],
         ),
         cost_estimate=pl.CostEstimate(
@@ -215,7 +218,7 @@
 def aligned_body(px, py, spectrum, concentration, factor_y, factor_x):
     k_local = spectrum.shape[1]
     x_local, line_total = concentration.shape
-    y_local, rank = factor_y.shape
+    y_local, _ = factor_y.shape
     planes = line_total // y_local
     sets = planes // py
     width = line_total // px
@@ -254,8 +257,12 @@
         for at, j in enumerate(group):
             velocity[j] = (whole, at)
 
-    y_parts, core_parts = [], []
-    for group in back_groups:
+    s_local = factor_x.shape[1] // px
+    factor_s = jnp.concatenate(
+        [lax.dynamic_slice_in_dim(factor_x, blocks[s] * s_local, s_local, 1) for s in range(px)], axis=1
+    )
+    y_parts, cores, core_parts = [], [], []
+    for g, group in enumerate(back_groups):
         whole, first = velocity[group[0]]
         rows = slice(first * rows_set, (first + len(group)) * rows_set)
         own = whole[rows]
@@ -263,7 +270,6 @@
         parts[0] = own[:, :x_local]
         for s in order:
             parts[s] = exchange(own[:, s * x_local : (s + 1) * x_local], "px", px, s)
-        cores = []
         for place, j in enumerate(group):
             sums = contract_flux(parts, place, conc[j], factor, me_y, py)
             total = sums[0]
@@ -272,17 +278,22 @@
             y_parts.append(total.T)
             cores.append(
                 lax.dot_general(
-                    factor_x,
+                    factor_s,
                     total,
                     (((0,), (1,)), ((), ())),
                     precision=HIGHEST,
                     preferred_element_type=jnp.float32,
                 )
             )
-        s_local = factor_x.shape[1] // px
-        terms = jnp.stack(cores).reshape(len(group), px, s_local, rank).transpose(1, 0, 2, 3)
-        terms = lax.all_to_all(terms, "px", split_axis=0, concat_axis=0, tiled=True)
-        core_parts.append(jnp.sum(terms, axis=0))
+        if g >= len(back_groups) - 2:
+            terms = [
+                jnp.stack([c[s * s_local : (s + 1) * s_local] for c in cores]) for s in range(px)
+            ]
+            summed = terms[0]
+            for s in order:
+                summed = summed + exchange(terms[s], "px", px, s)
+            core_parts.append(summed)
+            cores = []
     return jnp.stack(y_parts), jnp.concatenate(core_parts, axis=0)
 
 

time: 549 us -> 560 us (1.020)
  starting transfers between devices: 168 us -> 238 us
  waiting for transfers between devices: 158 us -> 99 us
  local copies, waits for them, and re-layouts: 31.8 us -> 24.5 us
    ppermute x47 -> x61, starting transfers between devices: 153 us -> 238 us  [exchange(): return lax.ppermute(value, axis, [(a, a ^ offset) for a in range(size)])]
    ppermute x47 -> x61, waiting for transfers between devices: 145 us -> 99 us  [exchange(): return lax.ppermute(value, axis, [(a, a ^ offset) for a in range(size)])]
    all_to_all x3 -> x0, starting transfers between devices: 15.1 us -> none  [aligned_body(): terms = lax.all_to_all(terms, 'px', split_axis=0, concat_axis=0, tiled=True)]
    all_to_all x3 -> x0, waiting for transfers between devices: 12.7 us -> none  [aligned_body(): terms = lax.all_to_all(terms, 'px', split_axis=0, concat_axis=0, tiled=True)]
    unnamed x93 -> x113, local copies, waits for them, and re-layouts: 15.9 us -> 13.6 us
  transfers between devices with their start and end apart: 50 -> 61, of which waited for: 14 -> 16; matrix products, arithmetic and copies ran while one was open for 19% -> 18% of each run, Pallas kernels for 18% -> 18%
where the time goes in v1:
time: 560 us; the launch traced here: 558 us
  starting transfers between devices  238 us (42%)
  Pallas kernels  106 us (19%)
  waiting for transfers between devices  99 us (18%)
  matrix products  64.8 us (12%)
  local copies, waits for them, and re-layouts  24.5 us (4%)
  other arithmetic  13.9 us (2%)
  between operations  11.4 us (2%)
    ppermute x61, starting transfers between devices, exchange(): return lax.ppermute(value, axis, [(a, a ^ offset) for a in range(size)])  238 us
    ppermute x61, waiting for transfers between devices, exchange(): return lax.ppermute(value, axis, [(a, a ^ offset) for a in range(size)])  99 us
    dot_general x2, matrix products, aligned_body(): lax.dot_general(lines, table, (((1,), (0,)), ((), ())), precision=lax.Pre...  61.5 us
    pallas_call x8, Pallas kernels, pack_peer(): pl.pallas_call(functools.partial(pack_kernel, planes, groups), out_shape=...  32.4 us
    pallas_call x1, Pallas kernels, build_table(): pl.pallas_call(table_kernel, out_shape=jax.ShapeDtypeStruct((2 * modes, g...  31.7 us
    pallas_call x4, Pallas kernels, contract_flux(): pl.pallas_call(functools.partial(flux_kernel, peers), out_shape=[jax.Shap...  23.4 us
    pallas_call x1, Pallas kernels, pack_all(): pl.pallas_call(functools.partial(pack_kernel, planes, groups), out_shape=...  18.9 us
    unnamed x113, local copies, waits for them, and re-layouts  13.6 us
  transfers between devices with their start and end apart: 61, of which 16 were waited for; matrix products, arithmetic and copies ran while one was open for 18% of the time, Pallas kernels for 18%

profile of v1, /device:TPU:0, one launch (start us, length us, event | category | flops | bytes accessed | tf_op | source)
XLA Modules:
  0.0 558.5 jit_solution(6617210134841455905)
XLA Ops:
  34.9 5.2 sine_multiply_fusion
  63.0 18.9 %pack_all.1 = (f32[8,192,384]{2,1,0:T(8,128)}, f32[8,192,384]{2,1,0:T(8,128)}, f32[8,192,384]{2,1,0:T(8,128)}, f32[8,192,384]{2,1,0:T(8,128)}) custom-call(s32[8]{0:T(128)} %copy-done.34, f32[384,6144]{1,0:T(8,128)} %in_ref.1), custom_call_target="tpu_custom_call" | custom-call | bytes 18874368 | tf_op jit(solution)/shard_map/pack_all/pallas_call | solution.py:112
  83.7 31.7 %build_table.1 = f32[3072,3072]{1,0:T(8,128)} custom-call(f32[8,192,24]{2,1,0:T(8,128)} %get-tuple-element.105.cos_far, f32[8,192,24]{2,1,0:T(8,128)} %get-tuple-element.104.sin_far, f32[8,192,128]{2,1,0:T(8,128)} %get-tuple-element.154.cos_near, f32[8,192,128]{2,1,0:T(8,128)} %get-tuple-element.153.sin_near), custom_call_target="tpu_custom_call" | custom-call | flops 28311552 | bytes 37748736 | tf_op jit(solution)/shard_map/build_table/pallas_call | solution.py:164
  135.7 25.4 %collective-permute-start.3 = (f32[384,384]{1,0:T(8,128)S(1)}, f32[384,384]{1,0:T(8,128)S(1)}, u32[]{:S(2)}, u32[]{:S(2)}) collective-permute-start(f32[384,384]{1,0:T(8,128)S(1)} %copy-done.38), channel_id=1, source_target_pairs={{0,16},{4,20},{8,24},{12,28},{16,0},{20,4},{24,8},{28,12},{1,17},{... | collective-permute-start | bytes 1769480 | tf_op jit(solution)/shard_map/ppermute | solution.py:17
  161.9 35.5 %collective-permute-start.4 = (f32[384,384]{1,0:T(8,128)S(1)}, f32[384,384]{1,0:T(8,128)S(1)}, u32[]{:S(2)}, u32[]{:S(2)}) collective-permute-start(f32[384,384]{1,0:T(8,128)S(1)} %copy-done.37), channel_id=1, source_target_pairs={{0,20},{4,16},{8,28},{12,24},{16,4},{20,0},{24,12},{28,8},{1,21},{... | collective-permute-start | bytes 1769480 | tf_op jit(solution)/shard_map/ppermute | solution.py:17
  198.4 29.9 %fusion.26 = f32[384,3072]{1,0:T(8,128)S(1)} fusion(f32[384,3072]{1,0:T(8,128)} %constant_dynamic-update-slice_fusion.8, f32[3072,3072]{1,0:T(8,128)} %build_table.1), kind=kOutput, calls=%fused_computation.119 | convolution fusion | flops 21743271936 | bytes 47185920 | tf_op jit(solution)/shard_map/dot_general | solution.py:250
  236.1 18.8 %collective-permute-done.4 = f32[384,384]{1,0:T(8,128)S(1)} collective-permute-done((f32[384,384]{1,0:T(8,128)S(1)}, f32[384,384]{1,0:T(8,128)S(1)}, u32[]{:S(2)}, u32[]{:S(2)}) %collective-permute-start.4) | collective-permute-done | bytes 589856 | tf_op jit(solution)/shard_map/ppermute | solution.py:17
  255.1 17.7 %collective-permute-start.40 = (f32[192,384]{1,0:T(8,128)S(1)}, f32[192,384]{1,0:T(8,128)S(1)}, u32[]{:S(2)}, u32[]{:S(2)}) collective-permute-start(f32[192,384]{1,0:T(8,128)S(1)} %get-tuple-element.92), channel_id=1, source_target_pairs={{0,16},{4,20},{8,24},{12,28},{16,0},{20,4},{24,8},{28,12},{1,17},{... | collective-permute-start | bytes 884744 | tf_op jit(solution)/shard_map/ppermute | solution.py:17
  272.8 16.7 %collective-permute-start.41 = (f32[192,384]{1,0:T(8,128)S(1)}, f32[192,384]{1,0:T(8,128)S(1)}, u32[]{:S(2)}, u32[]{:S(2)}) collective-permute-start(f32[192,384]{1,0:T(8,128)S(1)} %get-tuple-element.91), channel_id=1, source_target_pairs={{0,20},{4,16},{8,28},{12,24},{16,4},{20,0},{24,12},{28,8},{1,21},{... | collective-permute-start | bytes 884744 | tf_op jit(solution)/shard_map/ppermute | solution.py:17
  295.2 16.4 %collective-permute-done.40.refs_4_ = f32[192,384]{1,0:T(8,128)S(1)} collective-permute-done((f32[192,384]{1,0:T(8,128)S(1)}, f32[192,384]{1,0:T(8,128)S(1)}, u32[]{:S(2)}, u32[]{:S(2)}) %collective-permute-start.40) | collective-permute-done | bytes 294944 | tf_op jit(solution)/shard_map/ppermute | solution.py:17
  312.0 6.2 %collective-permute-done.41.refs_5_ = f32[192,384]{1,0:T(8,128)S(1)} collective-permute-done((f32[192,384]{1,0:T(8,128)S(1)}, f32[192,384]{1,0:T(8,128)S(1)}, u32[]{:S(2)}, u32[]{:S(2)}) %collective-permute-start.41) | collective-permute-done | bytes 294944 | tf_op jit(solution)/shard_map/ppermute | solution.py:17
  318.4 8.6 %collective-permute-start.30 = (f32[192,384]{1,0:T(8,128)S(1)}, f32[192,384]{1,0:T(8,128)}, u32[]{:S(2)}, u32[]{:S(2)}) collective-permute-start(f32[192,384]{1,0:T(8,128)S(1)} %get-tuple-element.99), channel_id=1, source_target_pairs={{0,16},{4,20},{8,24},{12,28},{16,0},{20,4},{24,8},{28,12},{1,17},{... | collective-permute-start | bytes 884744 | tf_op jit(solution)/shard_map/ppermute | solution.py:17
  327.0 13.1 %collective-permute-start.31 = (f32[192,384]{1,0:T(8,128)S(1)}, f32[192,384]{1,0:T(8,128)}, u32[]{:S(2)}, u32[]{:S(2)}) collective-permute-start(f32[192,384]{1,0:T(8,128)S(1)} %get-tuple-element.98), channel_id=1, source_target_pairs={{0,20},{4,16},{8,28},{12,24},{16,4},{20,0},{24,12},{28,8},{1,21},{... | collective-permute-start | bytes 884744 | tf_op jit(solution)/shard_map/ppermute | solution.py:17
  340.2 31.6 %fusion.25 = f32[384,3072]{1,0:T(8,128)} fusion(f32[384,3072]{1,0:T(8,128)} %copy-done.26, f32[3072,3072]{1,0:T(8,128)} %build_table.1), kind=kOutput, calls=%fused_computation.118 | convolution fusion | flops 21743271936 | bytes 47185920 | tf_op jit(solution)/shard_map/dot_general | solution.py:250
  371.8 5.8 %contract_flux.7 = (f32[128,384]{1,0:T(8,128)}, f32[128,384]{1,0:T(8,128)}, f32[128,384]{1,0:T(8,128)}, f32[128,384]{1,0:T(8,128)}) custom-call(s32[1]{0:T(128)} %bitcast.index_ref, f32[192,384]{1,0:T(8,128)} %get-tuple-element.96.refs_0_, f32[192,384]{1,0:T(8,128)} %copy-done.12, f32[192,384]{1,0:T(8,128)} %copy-done.14, f32[192,384]{1,0:T(8,128)} %copy-done.15, ...), custom_call_target="tpu_custom_call" | custom-call | flops 150994944 | bytes 4718592 | tf_op jit(solution)/shard_map/contract_flux/pallas_call | solution.py:192
  387.9 17.8 %collective-permute-start.10 = (f32[384,384]{1,0:T(8,128)}, f32[384,384]{1,0:T(8,128)S(1)}, u32[]{:S(2)}, u32[]{:S(2)}) collective-permute-start(f32[384,384]{1,0:T(8,128)} %get-tuple-element.83), channel_id=1, source_target_pairs={{0,16},{4,20},{8,24},{12,28},{16,0},{20,4},{24,8},{28,12},{1,17},{... | collective-permute-start | bytes 1769480 | tf_op jit(solution)/shard_map/ppermute | solution.py:17
  405.8 19.9 %collective-permute-start.11 = (f32[384,384]{1,0:T(8,128)}, f32[384,384]{1,0:T(8,128)S(1)}, u32[]{:S(2)}, u32[]{:S(2)}) collective-permute-start(f32[384,384]{1,0:T(8,128)} %get-tuple-element.82), channel_id=1, source_target_pairs={{0,20},{4,16},{8,28},{12,24},{16,4},{20,0},{24,12},{28,8},{1,21},{... | collective-permute-start | bytes 1769480 | tf_op jit(solution)/shard_map/ppermute | solution.py:17
  425.6 5.8 %contract_flux.6 = (f32[128,384]{1,0:T(8,128)}, f32[128,384]{1,0:T(8,128)}, f32[128,384]{1,0:T(8,128)}, f32[128,384]{1,0:T(8,128)}) custom-call(s32[1]{0:T(128)} %bitcast.index_ref, f32[192,384]{1,0:T(8,128)} %get-tuple-element.103.refs_0_, f32[192,384]{1,0:T(8,128)} %copy-done.11, f32[192,384]{1,0:T(8,128)} %copy-done.13, ...), custom_call_target="tpu_custom_call" | custom-call | flops 150994944 | bytes 4718592 | tf_op jit(solution)/shard_map/contract_flux/pallas_call | solution.py:192
  443.1 24.4 %collective-permute-done.54 = f32[1,32,128]{2,1,0:T(8,128)S(1)} collective-permute-done((f32[1,32,128]{2,1,0:T(8,128)S(1)}, f32[1,32,128]{2,1,0:T(8,128)S(1)}, u32[]{:S(2)}, u32[]{:S(2)}) %collective-permute-start.54) | collective-permute-done | bytes 16416 | tf_op jit(solution)/shard_map/ppermute | solution.py:17
  467.5 10.1 %collective-permute-start.13 = (f32[384,384]{1,0:T(8,128)}, f32[384,384]{1,0:T(8,128)S(1)}, u32[]{:S(2)}, u32[]{:S(2)}) collective-permute-start(f32[384,384]{1,0:T(8,128)} %get-tuple-element.80), channel_id=1, source_target_pairs={{0,28},{4,24},{8,20},{12,16},{16,12},{20,8},{24,4},{28,0},{1,29},{... | collective-permute-start | bytes 1769480 | tf_op jit(solution)/shard_map/ppermute | solution.py:17
  483.3 8.6 %collective-permute-done.13.refs_7_ = f32[384,384]{1,0:T(8,128)S(1)} collective-permute-done((f32[384,384]{1,0:T(8,128)}, f32[384,384]{1,0:T(8,128)S(1)}, u32[]{:S(2)}, u32[]{:S(2)}) %collective-permute-start.13) | collective-permute-done | bytes 589856 | tf_op jit(solution)/shard_map/ppermute | solution.py:17
  500.1 13.7 %collective-permute-start.59 = (f32[1,32,128]{2,1,0:T(8,128)}, f32[1,32,128]{2,1,0:T(8,128)}, u32[]{:S(2)}, u32[]{:S(2)}) collective-permute-start(f32[1,32,128]{2,1,0:T(8,128)} %get-tuple-element.148), channel_id=1, source_target_pairs={{0,8},{4,12},{8,0},{12,4},{16,24},{20,28},{24,16},{28,20},{1,9},{5... | collective-permute-start | bytes 49160 | tf_op jit(solution)/shard_map/ppermute | solution.py:17
  514.8 5.8 %contract_flux.4 = (f32[128,384]{1,0:T(8,128)}, f32[128,384]{1,0:T(8,128)}, f32[128,384]{1,0:T(8,128)}, f32[128,384]{1,0:T(8,128)}) custom-call(s32[1]{0:T(128)} %bitcast.index_ref, f32[384,384]{1,0:T(8,128)} %get-tuple-element.87.refs_0_, f32[384,384]{1,0:T(8,128)} %copy-done.5, f32[384,384]{1,0:T(8,128)} %collective-permute-done.8.refs_2_, ...), custom_call_target="tpu_custom_call" | custom-call | flops 150994944 | bytes 4718592 | tf_op jit(solution)/shard_map/contract_flux/pallas_call | solution.py:192
  523.5 6.1 %contract_flux.5 = (f32[128,384]{1,0:T(8,128)}, f32[128,384]{1,0:T(8,128)}, f32[128,384]{1,0:T(8,128)}, f32[128,384]{1,0:T(8,128)}) custom-call(s32[1]{0:T(128)} %bitcast.index_ref, f32[384,384]{1,0:T(8,128)} %get-tuple-element.87.refs_0_, f32[384,384]{1,0:T(8,128)} %copy-done.5, f32[384,384]{1,0:T(8,128)} %collective-permute-done.8.refs_2_, ...), custom_call_target="tpu_custom_call" | custom-call | flops 150994944 | bytes 4718592 | tf_op jit(solution)/shard_map/contract_flux/pallas_call | solution.py:192
  (271 shorter events, 153.4 us)
Async XLA Ops:
  5.4 111.9 %collective-permute-start.20 = (f32[384,384]{1,0:T(8,128)}, f32[384,384]{1,0:T(8,128)}, u32[]{:S(2)}, u32[]{:S(2)}) collective-permute-start(f32[384,384]{1,0:T(8,128)} %get-tuple-element.57), channel_id=1, source_target_pairs={{0,4},{4,0},{8,12},{12,8},{16,20},{20,16},{24,28},{28,24},{1,5},{5... | collective-permute-start | bytes 1769480 | tf_op jit(solution)/shard_map/ppermute | solution.py:17
  12.5 110.4 %collective-permute-start.21 = (f32[384,384]{1,0:T(8,128)}, f32[384,384]{1,0:T(8,128)}, u32[]{:S(2)}, u32[]{:S(2)}) collective-permute-start(f32[384,384]{1,0:T(8,128)} %get-tuple-element.58), channel_id=1, source_target_pairs={{0,8},{4,12},{8,0},{12,4},{16,24},{20,28},{24,16},{28,20},{1,9},{5... | collective-permute-start | bytes 1769480 | tf_op jit(solution)/shard_map/ppermute | solution.py:17
  18.1 106.7 %collective-permute-start.22 = (f32[384,384]{1,0:T(8,128)}, f32[384,384]{1,0:T(8,128)}, u32[]{:S(2)}, u32[]{:S(2)}) collective-permute-start(f32[384,384]{1,0:T(8,128)} %get-tuple-element.59), channel_id=1, source_target_pairs={{0,12},{4,8},{8,4},{12,0},{16,28},{20,24},{24,20},{28,16},{1,13},{... | collective-permute-start | bytes 1769480 | tf_op jit(solution)/shard_map/ppermute | solution.py:17
  22.2 106.3 %collective-permute-start.23 = (f32[384,384]{1,0:T(8,128)}, f32[384,384]{1,0:T(8,128)S(1)}, u32[]{:S(2)}, u32[]{:S(2)}) collective-permute-start(f32[384,384]{1,0:T(8,128)} %get-tuple-element.60), channel_id=1, source_target_pairs={{0,16},{4,20},{8,24},{12,28},{16,0},{20,4},{24,8},{28,12},{1,17},{... | collective-permute-start | bytes 1769480 | tf_op jit(solution)/shard_map/ppermute | solution.py:17
  29.2 100.2 %collective-permute-start.24 = (f32[384,384]{1,0:T(8,128)}, f32[384,384]{1,0:T(8,128)S(1)}, u32[]{:S(2)}, u32[]{:S(2)}) collective-permute-start(f32[384,384]{1,0:T(8,128)} %get-tuple-element.61), channel_id=1, source_target_pairs={{0,20},{4,16},{8,28},{12,24},{16,4},{20,0},{24,12},{28,8},{1,21},{... | collective-permute-start | bytes 1769480 | tf_op jit(solution)/shard_map/ppermute | solution.py:17
  124.8 103.5 %collective-permute-start = (f32[384,384]{1,0:T(8,128)S(1)}, f32[384,384]{1,0:T(8,128)S(1)}, u32[]{:S(2)}, u32[]{:S(2)}) collective-permute-start(f32[384,384]{1,0:T(8,128)S(1)} %copy-done.41), channel_id=1, source_target_pairs={{0,4},{4,0},{8,12},{12,8},{16,20},{20,16},{24,28},{28,24},{1,5},{5... | collective-permute-start | bytes 1769480 | tf_op jit(solution)/shard_map/ppermute | solution.py:17
  128.5 104.0 %collective-permute-start.1 = (f32[384,384]{1,0:T(8,128)S(1)}, f32[384,384]{1,0:T(8,128)S(1)}, u32[]{:S(2)}, u32[]{:S(2)}) collective-permute-start(f32[384,384]{1,0:T(8,128)S(1)} %copy-done.40), channel_id=1, source_target_pairs={{0,8},{4,12},{8,0},{12,4},{16,24},{20,28},{24,16},{28,20},{1,9},{5... | collective-permute-start | bytes 1769480 | tf_op jit(solution)/shard_map/ppermute | solution.py:17
  129.4 105.7 %collective-permute-start.2 = (f32[384,384]{1,0:T(8,128)S(1)}, f32[384,384]{1,0:T(8,128)S(1)}, u32[]{:S(2)}, u32[]{:S(2)}) collective-permute-start(f32[384,384]{1,0:T(8,128)S(1)} %copy-done.39), channel_id=1, source_target_pairs={{0,12},{4,8},{8,4},{12,0},{16,28},{20,24},{24,20},{28,16},{1,13},{... | collective-permute-start | bytes 1769480 | tf_op jit(solution)/shard_map/ppermute | solution.py:17
  135.7 100.2 %collective-permute-start.3 = (f32[384,384]{1,0:T(8,128)S(1)}, f32[384,384]{1,0:T(8,128)S(1)}, u32[]{:S(2)}, u32[]{:S(2)}) collective-permute-start(f32[384,384]{1,0:T(8,128)S(1)} %copy-done.38), channel_id=1, source_target_pairs={{0,16},{4,20},{8,24},{12,28},{16,0},{20,4},{24,8},{28,12},{1,17},{... | collective-permute-start | bytes 1769480 | tf_op jit(solution)/shard_map/ppermute | solution.py:17
  161.9 93.0 %collective-permute-start.4 = (f32[384,384]{1,0:T(8,128)S(1)}, f32[384,384]{1,0:T(8,128)S(1)}, u32[]{:S(2)}, u32[]{:S(2)}) collective-permute-start(f32[384,384]{1,0:T(8,128)S(1)} %copy-done.37), channel_id=1, source_target_pairs={{0,20},{4,16},{8,28},{12,24},{16,4},{20,0},{24,12},{28,8},{1,21},{... | collective-permute-start | bytes 1769480 | tf_op jit(solution)/shard_map/ppermute | solution.py:17
  235.0 54.5 %collective-permute-start.37 = (f32[192,384]{1,0:T(8,128)S(1)}, f32[192,384]{1,0:T(8,128)S(1)}, u32[]{:S(2)}, u32[]{:S(2)}) collective-permute-start(f32[192,384]{1,0:T(8,128)S(1)} %get-tuple-element.95), channel_id=1, source_target_pairs={{0,4},{4,0},{8,12},{12,8},{16,20},{20,16},{24,28},{28,24},{1,5},{5... | collective-permute-start | bytes 884744 | tf_op jit(solution)/shard_map/ppermute | solution.py:17
  235.9 54.3 %collective-permute-start.38 = (f32[192,384]{1,0:T(8,128)S(1)}, f32[192,384]{1,0:T(8,128)S(1)}, u32[]{:S(2)}, u32[]{:S(2)}) collective-permute-start(f32[192,384]{1,0:T(8,128)S(1)} %get-tuple-element.94), channel_id=1, source_target_pairs={{0,8},{4,12},{8,0},{12,4},{16,24},{20,28},{24,16},{28,20},{1,9},{5... | collective-permute-start | bytes 884744 | tf_op jit(solution)/shard_map/ppermute | solution.py:17
  255.1 56.5 %collective-permute-start.40 = (f32[192,384]{1,0:T(8,128)S(1)}, f32[192,384]{1,0:T(8,128)S(1)}, u32[]{:S(2)}, u32[]{:S(2)}) collective-permute-start(f32[192,384]{1,0:T(8,128)S(1)} %get-tuple-element.92), channel_id=1, source_target_pairs={{0,16},{4,20},{8,24},{12,28},{16,0},{20,4},{24,8},{28,12},{1,17},{... | collective-permute-start | bytes 884744 | tf_op jit(solution)/shard_map/ppermute | solution.py:17
  272.8 45.4 %collective-permute-start.41 = (f32[192,384]{1,0:T(8,128)S(1)}, f32[192,384]{1,0:T(8,128)S(1)}, u32[]{:S(2)}, u32[]{:S(2)}) collective-permute-start(f32[192,384]{1,0:T(8,128)S(1)} %get-tuple-element.91), channel_id=1, source_target_pairs={{0,20},{4,16},{8,28},{12,24},{16,4},{20,0},{24,12},{28,8},{1,21},{... | collective-permute-start | bytes 884744 | tf_op jit(solution)/shard_map/ppermute | solution.py:17
  293.7 83.9 %collective-permute-start.27 = (f32[192,384]{1,0:T(8,128)S(1)}, f32[192,384]{1,0:T(8,128)S(1)}, u32[]{:S(2)}, u32[]{:S(2)}) collective-permute-start(f32[192,384]{1,0:T(8,128)S(1)} %get-tuple-element.102), channel_id=1, source_target_pairs={{0,4},{4,0},{8,12},{12,8},{16,20},{20,16},{24,28},{28,24},{1,5},{5... | collective-permute-start | bytes 884744 | tf_op jit(solution)/shard_map/ppermute | solution.py:17
  311.6 67.4 %collective-permute-start.28 = (f32[192,384]{1,0:T(8,128)S(1)}, f32[192,384]{1,0:T(8,128)S(1)}, u32[]{:S(2)}, u32[]{:S(2)}) collective-permute-start(f32[192,384]{1,0:T(8,128)S(1)} %get-tuple-element.101), channel_id=1, source_target_pairs={{0,8},{4,12},{8,0},{12,4},{16,24},{20,28},{24,16},{28,20},{1,9},{5... | collective-permute-start | bytes 884744 | tf_op jit(solution)/shard_map/ppermute | solution.py:17
  318.2 63.3 %collective-permute-start.29 = (f32[192,384]{1,0:T(8,128)S(1)}, f32[192,384]{1,0:T(8,128)}, u32[]{:S(2)}, u32[]{:S(2)}) collective-permute-start(f32[192,384]{1,0:T(8,128)S(1)} %get-tuple-element.100), channel_id=1, source_target_pairs={{0,12},{4,8},{8,4},{12,0},{16,28},{20,24},{24,20},{28,16},{1,13},{... | collective-permute-start | bytes 884744 | tf_op jit(solution)/shard_map/ppermute | solution.py:17
  318.4 63.1 %collective-permute-start.30 = (f32[192,384]{1,0:T(8,128)S(1)}, f32[192,384]{1,0:T(8,128)}, u32[]{:S(2)}, u32[]{:S(2)}) collective-permute-start(f32[192,384]{1,0:T(8,128)S(1)} %get-tuple-element.99), channel_id=1, source_target_pairs={{0,16},{4,20},{8,24},{12,28},{16,0},{20,4},{24,8},{28,12},{1,17},{... | collective-permute-start | bytes 884744 | tf_op jit(solution)/shard_map/ppermute | solution.py:17
  327.0 56.0 %collective-permute-start.31 = (f32[192,384]{1,0:T(8,128)S(1)}, f32[192,384]{1,0:T(8,128)}, u32[]{:S(2)}, u32[]{:S(2)}) collective-permute-start(f32[192,384]{1,0:T(8,128)S(1)} %get-tuple-element.98), channel_id=1, source_target_pairs={{0,20},{4,16},{8,28},{12,24},{16,4},{20,0},{24,12},{28,8},{1,21},{... | collective-permute-start | bytes 884744 | tf_op jit(solution)/shard_map/ppermute | solution.py:17
  381.5 50.0 %collective-permute-start.44 = (f32[128,384]{1,0:T(8,128)}, f32[128,384]{1,0:T(8,128)S(1)}, u32[]{:S(2)}, u32[]{:S(2)}) collective-permute-start(f32[128,384]{1,0:T(8,128)} %get-tuple-element.71), channel_id=1, source_target_pairs={{0,1},{1,0},{2,3},{3,2},{4,5},{5,4},{6,7},{7,6},{8,9},{9,8},{10,11... | collective-permute-start | bytes 589832 | tf_op jit(solution)/shard_map/ppermute | solution.py:17
  381.5 50.0 %collective-permute-start.45 = (f32[128,384]{1,0:T(8,128)}, f32[128,384]{1,0:T(8,128)S(1)}, u32[]{:S(2)}, u32[]{:S(2)}) collective-permute-start(f32[128,384]{1,0:T(8,128)} %get-tuple-element.72), channel_id=1, source_target_pairs={{0,2},{1,3},{2,0},{3,1},{4,6},{5,7},{6,4},{7,5},{8,10},{9,11},{10,... | collective-permute-start | bytes 589832 | tf_op jit(solution)/shard_map/ppermute | solution.py:17
  383.0 50.1 %collective-permute-start.46 = (f32[128,384]{1,0:T(8,128)}, f32[128,384]{1,0:T(8,128)}, u32[]{:S(2)}, u32[]{:S(2)}) collective-permute-start(f32[128,384]{1,0:T(8,128)} %get-tuple-element.73), channel_id=1, source_target_pairs={{0,3},{1,2},{2,1},{3,0},{4,7},{5,6},{6,5},{7,4},{8,11},{9,10},{10,... | collective-permute-start | bytes 589832 | tf_op jit(solution)/shard_map/ppermute | solution.py:17
  387.9 90.8 %collective-permute-start.10 = (f32[384,384]{1,0:T(8,128)}, f32[384,384]{1,0:T(8,128)S(1)}, u32[]{:S(2)}, u32[]{:S(2)}) collective-permute-start(f32[384,384]{1,0:T(8,128)} %get-tuple-element.83), channel_id=1, source_target_pairs={{0,16},{4,20},{8,24},{12,28},{16,0},{20,4},{24,8},{28,12},{1,17},{... | collective-permute-start | bytes 1769480 | tf_op jit(solution)/shard_map/ppermute | solution.py:17
  405.8 73.0 %collective-permute-start.11 = (f32[384,384]{1,0:T(8,128)}, f32[384,384]{1,0:T(8,128)S(1)}, u32[]{:S(2)}, u32[]{:S(2)}) collective-permute-start(f32[384,384]{1,0:T(8,128)} %get-tuple-element.82), channel_id=1, source_target_pairs={{0,20},{4,16},{8,28},{12,24},{16,4},{20,0},{24,12},{28,8},{1,21},{... | collective-permute-start | bytes 1769480 | tf_op jit(solution)/shard_map/ppermute | solution.py:17
  (82 other events, 1933.8 us)

commit v2 on v1

--- a/solution.py
+++ b/solution.py
@@ -218,7 +218,7 @@
 def aligned_body(px, py, spectrum, concentration, factor_y, factor_x):
     k_local = spectrum.shape[1]
     x_local, line_total = concentration.shape
-    y_local, _ = factor_y.shape
+    y_local, rank = factor_y.shape
     planes = line_total // y_local
     sets = planes // py
     width = line_total // px
@@ -258,9 +258,6 @@
             velocity[j] = (whole, at)
 
     s_local = factor_x.shape[1] // px
-    factor_s = jnp.concatenate(
-        [lax.dynamic_slice_in_dim(factor_x, blocks[s] * s_local, s_local, 1) for s in range(px)], axis=1
-    )
     y_parts, cores, core_parts = [], [], []
     for g, group in enumerate(back_groups):
         whole, first = velocity[group[0]]
@@ -278,21 +275,17 @@
             y_parts.append(total.T)
             cores.append(
                 lax.dot_general(
-                    factor_s,
+                    factor_x,
                     total,
                     (((0,), (1,)), ((), ())),
                     precision=HIGHEST,
                     preferred_element_type=jnp.float32,
                 )
             )
-        if g >= len(back_groups) - 2:
-            terms = [
-                jnp.stack([c[s * s_local : (s + 1) * s_local] for c in cores]) for s in range(px)
-            ]
-            summed = terms[0]
-            for s in order:
-                summed = summed + exchange(terms[s], "px", px, s)
-            core_parts.append(summed)
+        if g in (0, len(back_groups) - 1):
+            terms = jnp.stack(cores).reshape(len(cores), px, s_local, rank).transpose(1, 0, 2, 3)
+            terms = lax.all_to_all(terms, "px", split_axis=0, concat_axis=0, tiled=True)
+            core_parts.append(jnp.sum(terms, axis=0))
             cores = []
     return jnp.stack(y_parts), jnp.concatenate(core_parts, axis=0)
 

time: 560 us -> 547 us (0.977)
  starting transfers between devices: 238 us -> 161 us
  waiting for transfers between devices: 99 us -> 161 us
  local copies, waits for them, and re-layouts: 24.5 us -> 32.8 us
    ppermute x61 -> x47, starting transfers between devices: 238 us -> 147 us  [exchange(): return lax.ppermute(value, axis, [(a, a ^ offset) for a in range(size)])]
    ppermute x61 -> x47, waiting for transfers between devices: 99 us -> 152 us  [exchange(): return lax.ppermute(value, axis, [(a, a ^ offset) for a in range(size)])]
    all_to_all x0 -> x2, starting transfers between devices: none -> 14.4 us  [aligned_body(): terms = lax.all_to_all(terms, 'px', split_axis=0, concat_axis=0, tiled=True)]
    unnamed x113 -> x93, local copies, waits for them, and re-layouts: 13.6 us -> 22 us
    all_to_all x0 -> x2, waiting for transfers between devices: none -> 8.21 us  [aligned_body(): terms = lax.all_to_all(terms, 'px', split_axis=0, concat_axis=0, tiled=True)]
  transfers between devices with their start and end apart: 61 -> 49, of which waited for: 16 -> 15; matrix products, arithmetic and copies ran while one was open for 18% -> 20% of each run, Pallas kernels for 18% -> 18%
where the time goes in v2:
time: 547 us; the launch traced here: 544 us
  starting transfers between devices  161 us (29%)
  waiting for transfers between devices  161 us (29%)
  Pallas kernels  106 us (19%)
  matrix products  63 us (12%)
  local copies, waits for them, and re-layouts  32.8 us (6%)
  other arithmetic  13.9 us (3%)
  between operations  6.4 us (1%)
    ppermute x47, waiting for transfers between devices, exchange(): return lax.ppermute(value, axis, [(a, a ^ offset) for a in range(size)])  152 us
    ppermute x47, starting transfers between devices, exchange(): return lax.ppermute(value, axis, [(a, a ^ offset) for a in range(size)])  147 us
    dot_general x2, matrix products, aligned_body(): lax.dot_general(lines, table, (((1,), (0,)), ((), ())), precision=lax.Pre...  59.9 us
    pallas_call x8, Pallas kernels, pack_peer(): pl.pallas_call(functools.partial(pack_kernel, planes, groups), out_shape=...  32.5 us
    pallas_call x1, Pallas kernels, build_table(): pl.pallas_call(table_kernel, out_shape=jax.ShapeDtypeStruct((2 * modes, g...  31.8 us
    pallas_call x4, Pallas kernels, contract_flux(): pl.pallas_call(functools.partial(flux_kernel, peers), out_shape=[jax.Shap...  23.4 us
    unnamed x93, local copies, waits for them, and re-layouts  22 us
    pallas_call x1, Pallas kernels, pack_all(): pl.pallas_call(functools.partial(pack_kernel, planes, groups), out_shape=...  18.8 us
  transfers between devices with their start and end apart: 49, of which 15 were waited for; matrix products, arithmetic and copies ran while one was open for 20% of the time, Pallas kernels for 18%

profile of v2, /device:TPU:0, one launch (start us, length us, event | category | flops | bytes accessed | tf_op | source)
XLA Modules:
  0.0 544.3 jit_solution(11317569300412788313)
XLA Ops:
  34.9 5.2 sine_multiply_fusion
  52.3 31.8 %build_table.1 = f32[3072,3072]{1,0:T(8,128)} custom-call(f32[8,192,24]{2,1,0:T(8,128)} %get-tuple-element.107.cos_far, f32[8,192,24]{2,1,0:T(8,128)} %get-tuple-element.106.sin_far, f32[8,192,128]{2,1,0:T(8,128)} %get-tuple-element.117.cos_near, f32[8,192,128]{2,1,0:T(8,128)} %get-tuple-element.116.sin_near), custom_call_target="tpu_custom_call" | custom-call | flops 28311552 | bytes 37748736 | tf_op jit(solution)/shard_map/build_table/pallas_call | solution.py:164
  105.5 25.4 %collective-permute-start.3 = (f32[384,384]{1,0:T(8,128)S(1)}, f32[384,384]{1,0:T(8,128)S(1)}, u32[]{:S(2)}, u32[]{:S(2)}) collective-permute-start(f32[384,384]{1,0:T(8,128)S(1)} %copy-done.28), channel_id=1, source_target_pairs={{0,16},{4,20},{8,24},{12,28},{16,0},{20,4},{24,8},{28,12},{1,17},{... | collective-permute-start | bytes 1769480 | tf_op jit(solution)/shard_map/ppermute | solution.py:17
  131.8 35.5 %collective-permute-start.4 = (f32[384,384]{1,0:T(8,128)S(1)}, f32[384,384]{1,0:T(8,128)S(1)}, u32[]{:S(2)}, u32[]{:S(2)}) collective-permute-start(f32[384,384]{1,0:T(8,128)S(1)} %copy-done.27), channel_id=1, source_target_pairs={{0,20},{4,16},{8,28},{12,24},{16,4},{20,0},{24,12},{28,8},{1,21},{... | collective-permute-start | bytes 1769480 | tf_op jit(solution)/shard_map/ppermute | solution.py:17
  168.2 30.0 %fusion.13 = f32[384,3072]{1,0:T(8,128)S(1)} fusion(f32[384,3072]{1,0:T(8,128)} %constant_dynamic-update-slice_fusion.8, f32[3072,3072]{1,0:T(8,128)} %build_table.1), kind=kOutput, calls=%fused_computation.64 | convolution fusion | flops 21743271936 | bytes 47185920 | tf_op jit(solution)/shard_map/dot_general | solution.py:250
  207.0 17.8 %collective-permute-done.4 = f32[384,384]{1,0:T(8,128)S(1)} collective-permute-done((f32[384,384]{1,0:T(8,128)S(1)}, f32[384,384]{1,0:T(8,128)S(1)}, u32[]{:S(2)}, u32[]{:S(2)}) %collective-permute-start.4) | collective-permute-done | bytes 589856 | tf_op jit(solution)/shard_map/ppermute | solution.py:17
  225.0 17.7 %collective-permute-start.30 = (f32[192,384]{1,0:T(8,128)S(1)}, f32[192,384]{1,0:T(8,128)S(1)}, u32[]{:S(2)}, u32[]{:S(2)}) collective-permute-start(f32[192,384]{1,0:T(8,128)S(1)} %get-tuple-element.101), channel_id=1, source_target_pairs={{0,16},{4,20},{8,24},{12,28},{16,0},{20,4},{24,8},{28,12},{1,17},{... | collective-permute-start | bytes 884744 | tf_op jit(solution)/shard_map/ppermute | solution.py:17
  242.8 16.5 %collective-permute-start.31 = (f32[192,384]{1,0:T(8,128)S(1)}, f32[192,384]{1,0:T(8,128)S(1)}, u32[]{:S(2)}, u32[]{:S(2)}) collective-permute-start(f32[192,384]{1,0:T(8,128)S(1)} %get-tuple-element.100), channel_id=1, source_target_pairs={{0,20},{4,16},{8,28},{12,24},{16,4},{20,0},{24,12},{28,8},{1,21},{... | collective-permute-start | bytes 884744 | tf_op jit(solution)/shard_map/ppermute | solution.py:17
  264.8 16.6 %collective-permute-done.30.refs_4_ = f32[192,384]{1,0:T(8,128)S(1)} collective-permute-done((f32[192,384]{1,0:T(8,128)S(1)}, f32[192,384]{1,0:T(8,128)S(1)}, u32[]{:S(2)}, u32[]{:S(2)}) %collective-permute-start.30) | collective-permute-done | bytes 294944 | tf_op jit(solution)/shard_map/ppermute | solution.py:17
  281.8 29.8 %fusion.12 = f32[384,3072]{1,0:T(8,128)S(1)} fusion(f32[384,3072]{1,0:T(8,128)} %copy-done.25, f32[3072,3072]{1,0:T(8,128)} %build_table.1), kind=kOutput, calls=%fused_computation.63 | convolution fusion | flops 21743271936 | bytes 47185920 | tf_op jit(solution)/shard_map/dot_general | solution.py:250
  326.1 47.1 %collective-permute-done.40.refs_4_ = f32[192,384]{1,0:T(8,128)S(1)} collective-permute-done((f32[192,384]{1,0:T(8,128)S(1)}, f32[192,384]{1,0:T(8,128)S(1)}, u32[]{:S(2)}, u32[]{:S(2)}) %collective-permute-start.40) | collective-permute-done | bytes 294944 | tf_op jit(solution)/shard_map/ppermute | solution.py:17
  389.1 18.8 %pack_all.1 = (f32[8,192,384]{2,1,0:T(8,128)}, f32[8,192,384]{2,1,0:T(8,128)}, f32[8,192,384]{2,1,0:T(8,128)}, f32[8,192,384]{2,1,0:T(8,128)}) custom-call(s32[8]{0:T(128)} %copy-done.26, f32[384,6144]{1,0:T(8,128)} %in_ref.1), custom_call_target="tpu_custom_call" | custom-call | bytes 18874368 | tf_op jit(solution)/shard_map/pack_all/pallas_call | solution.py:112
  409.8 5.8 %contract_flux.6 = (f32[128,384]{1,0:T(8,128)}, f32[128,384]{1,0:T(8,128)}, f32[128,384]{1,0:T(8,128)}, f32[128,384]{1,0:T(8,128)}) custom-call(s32[1]{0:T(128)} %bitcast.index_ref, f32[192,384]{1,0:T(8,128)} %get-tuple-element.105.refs_0_, f32[192,384]{1,0:T(8,128)} %copy-done.8, f32[192,384]{1,0:T(8,128)} %copy-done.9, f32[192,384]{1,0:T(8,128)} %copy-done.10, ...), custom_call_target="tpu_custom_call" | custom-call | flops 150994944 | bytes 4718592 | tf_op jit(solution)/shard_map/contract_flux/pallas_call | solution.py:192
  417.5 5.8 %contract_flux.7 = (f32[128,384]{1,0:T(8,128)}, f32[128,384]{1,0:T(8,128)}, f32[128,384]{1,0:T(8,128)}, f32[128,384]{1,0:T(8,128)}) custom-call(s32[1]{0:T(128)} %bitcast.index_ref, f32[192,384]{1,0:T(8,128)} %get-tuple-element.98.refs_0_, f32[192,384]{1,0:T(8,128)} %copy-done.12, f32[192,384]{1,0:T(8,128)} %copy-done.13, f32[192,384]{1,0:T(8,128)} %copy-done.15, ...), custom_call_target="tpu_custom_call" | custom-call | flops 150994944 | bytes 4718592 | tf_op jit(solution)/shard_map/contract_flux/pallas_call | solution.py:192
  445.8 13.2 %collective-permute-done.13.refs_7_ = f32[384,384]{1,0:T(8,128)S(1)} collective-permute-done((f32[384,384]{1,0:T(8,128)}, f32[384,384]{1,0:T(8,128)S(1)}, u32[]{:S(2)}, u32[]{:S(2)}) %collective-permute-start.13) | collective-permute-done | bytes 589856 | tf_op jit(solution)/shard_map/ppermute | solution.py:17
  459.0 5.0 collective-permute-done.7.refs_1_
  464.0 6.6 %collective-permute-done.8.refs_2_ = f32[384,384]{1,0:T(8,128)} collective-permute-done((f32[384,384]{1,0:T(8,128)}, f32[384,384]{1,0:T(8,128)}, u32[]{:S(2)}, u32[]{:S(2)}) %collective-permute-start.8) | collective-permute-done | bytes 589856 | tf_op jit(solution)/shard_map/ppermute | solution.py:17
  470.6 18.3 %collective-permute-done.9.refs_3_ = f32[384,384]{1,0:T(8,128)} collective-permute-done((f32[384,384]{1,0:T(8,128)}, f32[384,384]{1,0:T(8,128)}, u32[]{:S(2)}, u32[]{:S(2)}) %collective-permute-start.9) | collective-permute-done | bytes 589856 | tf_op jit(solution)/shard_map/ppermute | solution.py:17
  489.0 6.0 %contract_flux.4 = (f32[128,384]{1,0:T(8,128)}, f32[128,384]{1,0:T(8,128)}, f32[128,384]{1,0:T(8,128)}, f32[128,384]{1,0:T(8,128)}) custom-call(s32[1]{0:T(128)} %bitcast.index_ref, f32[384,384]{1,0:T(8,128)} %get-tuple-element.89.refs_0_, f32[384,384]{1,0:T(8,128)} %copy-done.5, f32[384,384]{1,0:T(8,128)} %collective-permute-done.8.refs_2_, ...), custom_call_target="tpu_custom_call" | custom-call | flops 150994944 | bytes 4718592 | tf_op jit(solution)/shard_map/contract_flux/pallas_call | solution.py:192
  500.1 8.4 %all-to-all-start.1 = ((f32[8,2,32,128]{3,2,1,0:T(8,128)}), f32[8,2,32,128]{3,2,1,0:T(8,128)S(1)}, u32[]{:S(2)}, u32[]{:S(2)}) async-start(f32[8,2,32,128]{3,2,1,0:T(8,128)} %copy.57), calls=%async_computation.1 | async-start | bytes 524288 | tf_op jit(solution)/shard_map/all_to_all | solution.py:287
  508.5 5.8 %contract_flux.5 = (f32[128,384]{1,0:T(8,128)}, f32[128,384]{1,0:T(8,128)}, f32[128,384]{1,0:T(8,128)}, f32[128,384]{1,0:T(8,128)}) custom-call(s32[1]{0:T(128)} %bitcast.index_ref, f32[384,384]{1,0:T(8,128)} %get-tuple-element.89.refs_0_, f32[384,384]{1,0:T(8,128)} %copy-done.5, f32[384,384]{1,0:T(8,128)} %collective-permute-done.8.refs_2_, ...), custom_call_target="tpu_custom_call" | custom-call | flops 150994944 | bytes 4718592 | tf_op jit(solution)/shard_map/contract_flux/pallas_call | solution.py:192
  516.2 6.1 %collective-permute-done.18 = f32[128,384]{1,0:T(8,128)S(1)} collective-permute-done((f32[128,384]{1,0:T(8,128)}, f32[128,384]{1,0:T(8,128)S(1)}, u32[]{:S(2)}, u32[]{:S(2)}) %collective-permute-start.18) | collective-permute-done | bytes 196640 | tf_op jit(solution)/shard_map/ppermute | solution.py:17
  528.2 6.0 %all-to-all-start = ((f32[8,2,32,128]{3,2,1,0:T(8,128)}), f32[8,2,32,128]{3,2,1,0:T(8,128)S(1)}, u32[]{:S(2)}, u32[]{:S(2)}) async-start(f32[8,2,32,128]{3,2,1,0:T(8,128)} %copy.54), calls=%async_computation | async-start | bytes 524288 | tf_op jit(solution)/shard_map/all_to_all | solution.py:287
  535.4 8.2 %all-to-all-done = f32[8,2,32,128]{3,2,1,0:T(8,128)S(1)} async-done(((f32[8,2,32,128]{3,2,1,0:T(8,128)}), f32[8,2,32,128]{3,2,1,0:T(8,128)S(1)}, u32[]{:S(2)}, u32[]{:S(2)}) %all-to-all-start) | async-done | bytes 262176 | tf_op jit(solution)/shard_map/all_to_all | solution.py:287
  (222 shorter events, 150.5 us)
Async XLA Ops:
  5.4 81.7 %collective-permute-start.20 = (f32[384,384]{1,0:T(8,128)}, f32[384,384]{1,0:T(8,128)}, u32[]{:S(2)}, u32[]{:S(2)}) collective-permute-start(f32[384,384]{1,0:T(8,128)} %get-tuple-element.57), channel_id=1, source_target_pairs={{0,4},{4,0},{8,12},{12,8},{16,20},{20,16},{24,28},{28,24},{1,5},{5... | collective-permute-start | bytes 1769480 | tf_op jit(solution)/shard_map/ppermute | solution.py:17
  12.5 80.2 %collective-permute-start.21 = (f32[384,384]{1,0:T(8,128)}, f32[384,384]{1,0:T(8,128)}, u32[]{:S(2)}, u32[]{:S(2)}) collective-permute-start(f32[384,384]{1,0:T(8,128)} %get-tuple-element.58), channel_id=1, source_target_pairs={{0,8},{4,12},{8,0},{12,4},{16,24},{20,28},{24,16},{28,20},{1,9},{5... | collective-permute-start | bytes 1769480 | tf_op jit(solution)/shard_map/ppermute | solution.py:17
  18.2 76.4 %collective-permute-start.22 = (f32[384,384]{1,0:T(8,128)}, f32[384,384]{1,0:T(8,128)S(1)}, u32[]{:S(2)}, u32[]{:S(2)}) collective-permute-start(f32[384,384]{1,0:T(8,128)} %get-tuple-element.59), channel_id=1, source_target_pairs={{0,12},{4,8},{8,4},{12,0},{16,28},{20,24},{24,20},{28,16},{1,13},{... | collective-permute-start | bytes 1769480 | tf_op jit(solution)/shard_map/ppermute | solution.py:17
  22.2 75.0 %collective-permute-start.23 = (f32[384,384]{1,0:T(8,128)}, f32[384,384]{1,0:T(8,128)S(1)}, u32[]{:S(2)}, u32[]{:S(2)}) collective-permute-start(f32[384,384]{1,0:T(8,128)} %get-tuple-element.60), channel_id=1, source_target_pairs={{0,16},{4,20},{8,24},{12,28},{16,0},{20,4},{24,8},{28,12},{1,17},{... | collective-permute-start | bytes 1769480 | tf_op jit(solution)/shard_map/ppermute | solution.py:17
  29.2 68.9 %collective-permute-start.24 = (f32[384,384]{1,0:T(8,128)}, f32[384,384]{1,0:T(8,128)S(1)}, u32[]{:S(2)}, u32[]{:S(2)}) collective-permute-start(f32[384,384]{1,0:T(8,128)} %get-tuple-element.61), channel_id=1, source_target_pairs={{0,20},{4,16},{8,28},{12,24},{16,4},{20,0},{24,12},{28,8},{1,21},{... | collective-permute-start | bytes 1769480 | tf_op jit(solution)/shard_map/ppermute | solution.py:17
  94.6 103.6 %collective-permute-start = (f32[384,384]{1,0:T(8,128)S(1)}, f32[384,384]{1,0:T(8,128)S(1)}, u32[]{:S(2)}, u32[]{:S(2)}) collective-permute-start(f32[384,384]{1,0:T(8,128)S(1)} %copy-done.32), channel_id=1, source_target_pairs={{0,4},{4,0},{8,12},{12,8},{16,20},{20,16},{24,28},{28,24},{1,5},{5... | collective-permute-start | bytes 1769480 | tf_op jit(solution)/shard_map/ppermute | solution.py:17
  97.2 106.5 %collective-permute-start.1 = (f32[384,384]{1,0:T(8,128)S(1)}, f32[384,384]{1,0:T(8,128)S(1)}, u32[]{:S(2)}, u32[]{:S(2)}) collective-permute-start(f32[384,384]{1,0:T(8,128)S(1)} %copy-done.30), channel_id=1, source_target_pairs={{0,8},{4,12},{8,0},{12,4},{16,24},{20,28},{24,16},{28,20},{1,9},{5... | collective-permute-start | bytes 1769480 | tf_op jit(solution)/shard_map/ppermute | solution.py:17
  98.1 107.3 %collective-permute-start.2 = (f32[384,384]{1,0:T(8,128)S(1)}, f32[384,384]{1,0:T(8,128)S(1)}, u32[]{:S(2)}, u32[]{:S(2)}) collective-permute-start(f32[384,384]{1,0:T(8,128)S(1)} %copy-done.29), channel_id=1, source_target_pairs={{0,12},{4,8},{8,4},{12,0},{16,28},{20,24},{24,20},{28,16},{1,13},{... | collective-permute-start | bytes 1769480 | tf_op jit(solution)/shard_map/ppermute | solution.py:17
  105.5 101.4 %collective-permute-start.3 = (f32[384,384]{1,0:T(8,128)S(1)}, f32[384,384]{1,0:T(8,128)S(1)}, u32[]{:S(2)}, u32[]{:S(2)}) collective-permute-start(f32[384,384]{1,0:T(8,128)S(1)} %copy-done.28), channel_id=1, source_target_pairs={{0,16},{4,20},{8,24},{12,28},{16,0},{20,4},{24,8},{28,12},{1,17},{... | collective-permute-start | bytes 1769480 | tf_op jit(solution)/shard_map/ppermute | solution.py:17
  131.8 93.0 %collective-permute-start.4 = (f32[384,384]{1,0:T(8,128)S(1)}, f32[384,384]{1,0:T(8,128)S(1)}, u32[]{:S(2)}, u32[]{:S(2)}) collective-permute-start(f32[384,384]{1,0:T(8,128)S(1)} %copy-done.27), channel_id=1, source_target_pairs={{0,20},{4,16},{8,28},{12,24},{16,4},{20,0},{24,12},{28,8},{1,21},{... | collective-permute-start | bytes 1769480 | tf_op jit(solution)/shard_map/ppermute | solution.py:17
  205.5 54.0 %collective-permute-start.27 = (f32[192,384]{1,0:T(8,128)S(1)}, f32[192,384]{1,0:T(8,128)S(1)}, u32[]{:S(2)}, u32[]{:S(2)}) collective-permute-start(f32[192,384]{1,0:T(8,128)S(1)} %get-tuple-element.104), channel_id=1, source_target_pairs={{0,4},{4,0},{8,12},{12,8},{16,20},{20,16},{24,28},{28,24},{1,5},{5... | collective-permute-start | bytes 884744 | tf_op jit(solution)/shard_map/ppermute | solution.py:17
  206.9 53.3 %collective-permute-start.28 = (f32[192,384]{1,0:T(8,128)S(1)}, f32[192,384]{1,0:T(8,128)S(1)}, u32[]{:S(2)}, u32[]{:S(2)}) collective-permute-start(f32[192,384]{1,0:T(8,128)S(1)} %get-tuple-element.103), channel_id=1, source_target_pairs={{0,8},{4,12},{8,0},{12,4},{16,24},{20,28},{24,16},{28,20},{1,9},{5... | collective-permute-start | bytes 884744 | tf_op jit(solution)/shard_map/ppermute | solution.py:17
  225.0 56.5 %collective-permute-start.30 = (f32[192,384]{1,0:T(8,128)S(1)}, f32[192,384]{1,0:T(8,128)S(1)}, u32[]{:S(2)}, u32[]{:S(2)}) collective-permute-start(f32[192,384]{1,0:T(8,128)S(1)} %get-tuple-element.101), channel_id=1, source_target_pairs={{0,16},{4,20},{8,24},{12,28},{16,0},{20,4},{24,8},{28,12},{1,17},{... | collective-permute-start | bytes 884744 | tf_op jit(solution)/shard_map/ppermute | solution.py:17
  242.8 68.9 %collective-permute-start.31 = (f32[192,384]{1,0:T(8,128)S(1)}, f32[192,384]{1,0:T(8,128)S(1)}, u32[]{:S(2)}, u32[]{:S(2)}) collective-permute-start(f32[192,384]{1,0:T(8,128)S(1)} %get-tuple-element.100), channel_id=1, source_target_pairs={{0,20},{4,16},{8,28},{12,24},{16,4},{20,0},{24,12},{28,8},{1,21},{... | collective-permute-start | bytes 884744 | tf_op jit(solution)/shard_map/ppermute | solution.py:17
  259.5 54.2 %collective-permute-start.32 = (f32[192,384]{1,0:T(8,128)S(1)}, f32[192,384]{1,0:T(8,128)S(1)}, u32[]{:S(2)}, u32[]{:S(2)}) collective-permute-start(f32[192,384]{1,0:T(8,128)S(1)} %get-tuple-element.99), channel_id=1, source_target_pairs={{0,24},{4,28},{8,16},{12,20},{16,8},{20,12},{24,0},{28,4},{1,25},{... | collective-permute-start | bytes 884744 | tf_op jit(solution)/shard_map/ppermute | solution.py:17
  260.2 55.2 %collective-permute-start.33 = (f32[192,384]{1,0:T(8,128)S(1)}, f32[192,384]{1,0:T(8,128)S(1)}, u32[]{:S(2)}, u32[]{:S(2)}) collective-permute-start(f32[192,384]{1,0:T(8,128)S(1)} %get-tuple-element.90), channel_id=1, source_target_pairs={{0,28},{4,24},{8,20},{12,16},{16,12},{20,8},{24,4},{28,0},{1,29},{... | collective-permute-start | bytes 884744 | tf_op jit(solution)/shard_map/ppermute | solution.py:17
  263.4 53.9 %collective-permute-start.37 = (f32[192,384]{1,0:T(8,128)S(1)}, f32[192,384]{1,0:T(8,128)S(1)}, u32[]{:S(2)}, u32[]{:S(2)}) collective-permute-start(f32[192,384]{1,0:T(8,128)S(1)} %get-tuple-element.97), channel_id=1, source_target_pairs={{0,4},{4,0},{8,12},{12,8},{16,20},{20,16},{24,28},{28,24},{1,5},{5... | collective-permute-start | bytes 884744 | tf_op jit(solution)/shard_map/ppermute | solution.py:17
  313.7 59.5 %collective-permute-start.40 = (f32[192,384]{1,0:T(8,128)S(1)}, f32[192,384]{1,0:T(8,128)S(1)}, u32[]{:S(2)}, u32[]{:S(2)}) collective-permute-start(f32[192,384]{1,0:T(8,128)S(1)} %get-tuple-element.94), channel_id=1, source_target_pairs={{0,16},{4,20},{8,24},{12,28},{16,0},{20,4},{24,8},{28,12},{1,17},{... | collective-permute-start | bytes 884744 | tf_op jit(solution)/shard_map/ppermute | solution.py:17
  315.4 100.1 %collective-permute-start.41 = (f32[192,384]{1,0:T(8,128)S(1)}, f32[192,384]{1,0:T(8,128)S(1)}, u32[]{:S(2)}, u32[]{:S(2)}) collective-permute-start(f32[192,384]{1,0:T(8,128)S(1)} %get-tuple-element.93), channel_id=1, source_target_pairs={{0,20},{4,16},{8,28},{12,24},{16,4},{20,0},{24,12},{28,8},{1,21},{... | collective-permute-start | bytes 884744 | tf_op jit(solution)/shard_map/ppermute | solution.py:17
  317.3 98.4 %collective-permute-start.42 = (f32[192,384]{1,0:T(8,128)S(1)}, f32[192,384]{1,0:T(8,128)}, u32[]{:S(2)}, u32[]{:S(2)}) collective-permute-start(f32[192,384]{1,0:T(8,128)S(1)} %get-tuple-element.92), channel_id=1, source_target_pairs={{0,24},{4,28},{8,16},{12,20},{16,8},{20,12},{24,0},{28,4},{1,25},{... | collective-permute-start | bytes 884744 | tf_op jit(solution)/shard_map/ppermute | solution.py:17
  320.6 95.1 %collective-permute-start.43 = (f32[192,384]{1,0:T(8,128)S(1)}, f32[192,384]{1,0:T(8,128)}, u32[]{:S(2)}, u32[]{:S(2)}) collective-permute-start(f32[192,384]{1,0:T(8,128)S(1)} %get-tuple-element.91), channel_id=1, source_target_pairs={{0,28},{4,24},{8,20},{12,16},{16,12},{20,8},{24,4},{28,0},{1,29},{... | collective-permute-start | bytes 884744 | tf_op jit(solution)/shard_map/ppermute | solution.py:17
  323.6 112.8 %collective-permute-start.10 = (f32[384,384]{1,0:T(8,128)}, f32[384,384]{1,0:T(8,128)S(1)}, u32[]{:S(2)}, u32[]{:S(2)}) collective-permute-start(f32[384,384]{1,0:T(8,128)} %get-tuple-element.85), channel_id=1, source_target_pairs={{0,16},{4,20},{8,24},{12,28},{16,0},{20,4},{24,8},{28,12},{1,17},{... | collective-permute-start | bytes 1769480 | tf_op jit(solution)/shard_map/ppermute | solution.py:17
  373.2 64.5 %collective-permute-start.11 = (f32[384,384]{1,0:T(8,128)}, f32[384,384]{1,0:T(8,128)S(1)}, u32[]{:S(2)}, u32[]{:S(2)}) collective-permute-start(f32[384,384]{1,0:T(8,128)} %get-tuple-element.84), channel_id=1, source_target_pairs={{0,20},{4,16},{8,28},{12,24},{16,4},{20,0},{24,12},{28,8},{1,21},{... | collective-permute-start | bytes 1769480 | tf_op jit(solution)/shard_map/ppermute | solution.py:17
  437.7 51.3 %collective-permute-start.9 = (f32[384,384]{1,0:T(8,128)}, f32[384,384]{1,0:T(8,128)}, u32[]{:S(2)}, u32[]{:S(2)}) collective-permute-start(f32[384,384]{1,0:T(8,128)} %get-tuple-element.86), channel_id=1, source_target_pairs={{0,12},{4,8},{8,4},{12,0},{16,28},{20,24},{24,20},{28,16},{1,13},{... | collective-permute-start | bytes 1769480 | tf_op jit(solution)/shard_map/ppermute | solution.py:17
  (60 other events, 1783.0 us)
